TPU v7x, 128 devices: a whole 4x4x4 slice. The times are simulated.
128 devices in a mesh: ka: 8 (over y, z_lo), rp: 16 (over z_hi, x, core).
Axes of the slice: x: 4, y: 4, z: 4 (z_hi: 2, z_lo: 2; z = z_hi * 2 + z_lo), core: 2. Of those that a mesh axis runs over, the one named last changes fastest.
Arguments:
- coupling_table: bfloat16 [512, 256, 1024], P('ka', 'rp'), may hold values from -0.016479492 to 0.016479492
- k_points: int32 [3, 4096], P(None, 'ka'), may hold values from 0 to 15
- re_vectors: int32 [3, 512], replicated, may hold values from -6 to 6
- rp_vectors: int32 [3, 256], P(None, 'rp'), may hold values from -6 to 6
- q_points: int32 [3, 2], replicated, may hold values from 0 to 15
Outputs:
- bloch_coupling: float32 [4096, 2048], P(('ka', 'rp'))
All inputs are finite; a program needn't handle non-finite values.
Results may differ from a plain program's by a relative error of at most 0.0022.
Values may be sent and summed in bfloat16 or wider, within the bound.
No kernel may reach another device: no remote copies, remote signals or barrier semaphores. Data moves between devices by JAX's collectives and lax.ppermute only.
A program may use at most 64 MiB of HBM per device.

v0:
```python
import math

import jax
import jax.numpy as jnp
from jax import lax
from jax.sharding import PartitionSpec as P

NKG = 16


def phases(left, right):
    nested = (
        left[0][:, None] * right[0][None, :]
        + left[1][:, None] * right[1][None, :]
        + left[2][:, None] * right[2][None, :]
    )
    wrapped = jnp.mod(nested, NKG)
    angles = wrapped.astype(jnp.float32) * (2.0 * math.pi / NKG)
    return (jnp.cos(angles), jnp.sin(angles))


def per_device(coupling_table, k_points, re_vectors, rp_vectors, q_points):
    high = lax.Precision.HIGHEST
    local_rp = coupling_table.shape[1]
    entries = coupling_table.shape[2] // 2
    waves = q_points.shape[1]
    q_cos, q_sin = phases(q_points, rp_vectors)
    k_cos, k_sin = phases(k_points, re_vectors)
    k_cos = k_cos.astype(jnp.bfloat16)
    k_sin = k_sin.astype(jnp.bfloat16)
    local_re = coupling_table.shape[0]
    values = coupling_table.astype(jnp.float32).reshape(local_re, local_rp, 2, entries)
    real_in = values[:, :, 0, :]
    imag_in = values[:, :, 1, :]
    real_mid = jnp.einsum("qr,erm->eqm", q_cos, real_in, precision=high) - jnp.einsum(
        "qr,erm->eqm", q_sin, imag_in, precision=high
    )
    imag_mid = jnp.einsum("qr,erm->eqm", q_sin, real_in, precision=high) + jnp.einsum(
        "qr,erm->eqm", q_cos, imag_in, precision=high
    )
    stacked = jnp.stack(
        [real_mid.reshape(local_re, waves * entries), imag_mid.reshape(local_re, waves * entries)],
        axis=0,
    )
    reduced = lax.psum_scatter(stacked, "rp", scatter_dimension=2, tiled=True)
    fragment = lax.all_gather(reduced, "ka", axis=1, tiled=True)
    cos_part = k_cos.astype(jnp.float32)
    sin_part = k_sin.astype(jnp.float32)
    real_add = jnp.dot(
        cos_part, fragment[0], precision=high, preferred_element_type=jnp.float32
    ) - jnp.dot(sin_part, fragment[1], precision=high, preferred_element_type=jnp.float32)
    imag_add = jnp.dot(
        sin_part, fragment[0], precision=high, preferred_element_type=jnp.float32
    ) + jnp.dot(cos_part, fragment[1], precision=high, preferred_element_type=jnp.float32)
    combined = jnp.stack([real_add, imag_add], axis=1)
    moved = lax.all_to_all(combined, "rp", split_axis=0, concat_axis=2, tiled=True)
    return moved.reshape(moved.shape[0], 2 * waves * entries)


def solution(mesh):
    placed = (P("ka", "rp", None), P(None, "ka"), P(), P(None, "rp"), P())
    return jax.shard_map(
        per_device, mesh=mesh, in_specs=placed, out_specs=P(("ka", "rp"), None), check_vma=False
    )
```

profile of v0, /device:TPU:1, one launch (start us, length us, event | category | flops | bytes accessed | tf_op | source)
XLA Modules:
  0.0 165.0 jit_solution(7246096939877109903)
XLA Ops:
  6.5 0.8 slice_bitcast_fusion.8
  7.3 1.0 slice_reduce_fusion.2
  8.3 3.3 %reshape.13 = bf16[64,16,2,512]{3,2,1,0:T(2,128)(2,1)S(1)} reshape(bf16[64,16,1024]{2,1,0:T(8,128)(2,1)} %param.5) | data formatting | bytes 4194304 | tf_op jit(solution)/shard_map/reshape | solution.py:32
  11.7 4.5 %fusion.36 = (bf16[64,16,1,512]{3,2,1,0:T(2,128)(2,1)S(1)}, bf16[64,16,1,512]{3,2,1,0:T(2,128)(2,1)S(1)}) fusion(bf16[64,16,2,512]{3,2,1,0:T(2,128)(2,1)S(1)} %reshape.13), kind=kLoop, calls=%fused_computation.59 | loop fusion | bytes 4194304 | tf_op jit(solution)/shard_map/slice | solution.py:34
  16.2 0.1 fusion.34
  16.3 0.6 fusion.8
  16.9 0.6 fusion.7
  17.5 0.0 copy-done
  17.5 0.6 fusion.1
  18.1 0.2 stack_reshape.6
  18.3 2.2 %fusion = f32[64,2,512]{2,1,0:T(2,128)S(1)} fusion(f32[2,64,512]{2,0,1:T(2,128)S(1)} %fusion.7, bf16[64,16,1,512]{3,2,1,0:T(2,128)(2,1)} %copy-done, f32[2,16]{1,0:T(2,128)S(1)} %get-tuple-element.8), kind=kOutput, calls=%fused_computation.4 | convolution fusion | flops 12648448 | bytes 1572992 | tf_op jit(solution)/shard_map/qr,erm->eqm/dot_general | solution.py:38
  20.5 0.2 stack_reshape.7
  20.8 0.0 copy-start.2
  20.8 0.6 copy.19
  21.4 1.4 reshape.17
  22.7 0.0 reduce-scatter.4.cloned.1.call-update
  22.8 66.8 %reduce-scatter.4.cloned.1.call-done = f32[64,128]{1,0:T(8,128)} async-done(((f32[1024,128]{1,0:T(8,128)}), f32[64,128]{1,0:T(8,128)}) %reduce-scatter.4.cloned.1.call-update) | async-done | bytes 32784
  89.6 0.9 reshape.18
  90.5 0.1 copy.20
  90.5 23.7 %all_gather.3 = f32[2,512,64]{2,1,0:T(8,128)S(1)} all-gather(f32[2,64,64]{2,1,0:T(8,128)S(1)} %copy.20), channel_id=1, replica_groups=mesh['ka'=8,'rp'=16] {'ka'}, dimensions={1}, use_global_device_ids=true | all-gather | bytes 294912 | tf_op jit(solution)/shard_map/all_gather | solution.py:46
  114.3 4.5 %fusion.9 = f32[512,64]{0,1:T(8,128)S(1)} fusion(s32[512]{0:T(512)S(1)} %bitcast.72, s32[512]{0:T(512)S(1)} %bitcast.60, s32[512]{0:T(512)S(1)} %bitcast.76, s32[512]{0:T(512)S(1)} %bitcast.64, s32[512]{0:T(512)S(1)} %bitcast.68, s32[512]{0:T(512)S(1)} %bitcast.56, f32[2,512,64]{2,1,0:T(8,128)S(1)} %all_gather.3), kind=kOutput, calls=%fused_computation.21 | convolution fusion | flops 206307328 | bytes 405504 | tf_op jit(solution)/shard_map/dot_general | solution.py:49
  118.8 4.5 %fusion.10 = f32[512,64]{0,1:T(8,128)S(1)} fusion(s32[512]{0:T(512)S(1)} %bitcast.73, s32[512]{0:T(512)S(1)} %bitcast.61, s32[512]{0:T(512)S(1)} %bitcast.77, s32[512]{0:T(512)S(1)} %bitcast.65, s32[512]{0:T(512)S(1)} %bitcast.69, s32[512]{0:T(512)S(1)} %bitcast.57, f32[2,512,64]{2,1,0:T(8,128)S(1)} %all_gather.3), kind=kOutput, calls=%fused_computation.22 | convolution fusion | flops 206307328 | bytes 405504 | tf_op jit(solution)/shard_map/dot_general | solution.py:52
  123.3 4.7 %fusion.3 = f32[512,1,64]{0,2,1:T(8,128)S(1)} fusion(f32[512,64]{0,1:T(8,128)S(1)} %fusion.9, s32[512]{0:T(512)S(1)} %bitcast.74, s32[512]{0:T(512)S(1)} %bitcast.62, s32[512]{0:T(512)S(1)} %bitcast.78, s32[512]{0:T(512)S(1)} %bitcast.66, s32[512]{0:T(512)S(1)} %bitcast.70, s32[512]{0:T(512)S(1)} %bitcast.58, f32[2,512,64]{2,1,0:T(8,128)S(1)} %all_gather.3), kind=kOutput, calls=%fused_computation.10 | convolution fusion | flops 206340096 | bytes 536576 | tf_op jit(solution)/shard_map/dot_general | solution.py:51
  128.0 4.5 %fusion.2 = f32[512,1,64]{0,2,1:T(8,128)S(1)} fusion(f32[512,64]{0,1:T(8,128)S(1)} %fusion.10, s32[512]{0:T(512)S(1)} %bitcast.75, s32[512]{0:T(512)S(1)} %bitcast.63, s32[512]{0:T(512)S(1)} %bitcast.79, s32[512]{0:T(512)S(1)} %bitcast.67, s32[512]{0:T(512)S(1)} %bitcast.71, s32[512]{0:T(512)S(1)} %bitcast.59, f32[2,512,64]{2,1,0:T(8,128)S(1)} %all_gather.3), kind=kOutput, calls=%fused_computation.8 | convolution fusion | flops 206340096 | bytes 536576 | tf_op jit(solution)/shard_map/dot_general | solution.py:54
  132.6 0.2 copy.16
  132.8 0.6 reshape.22
  133.4 21.3 %all_to_all.15 = f32[16,1,4096]{2,1,0:T(1,128)S(1)} all-to-all(f32[16,1,4096]{2,1,0:T(1,128)S(1)} %reshape.22), channel_id=1, replica_groups=mesh['ka'=8,'rp'=16] {'rp'}, dimensions={0} | all-to-all | bytes 524288 | tf_op jit(solution)/shard_map/all_to_all | solution.py:56
  154.7 0.5 broadcast.28
  155.2 1.3 reduce.6
  156.5 0.4 reshape.23
  156.9 0.3 copy.18
  157.2 0.9 reshape.14
  (11 shorter events, 0.2 us)
Async XLA Ops:
  6.5 83.1 %reduce-scatter.4.cloned.1.call-start = ((), (), s32[]{:S(2)}) async-start(), calls=%async_computation.2 | async-start | bytes 557056
  16.2 1.4 copy-start
  20.8 2.0 %copy-start.1 = (s32[3,512]{1,0:T(4,128)S(1)}, s32[3,512]{1,0:T(4,128)}, u32[]{:S(2)}) copy-start(s32[3,512]{1,0:T(4,128)} %param.6) | copy-start | bytes 18436
  20.8 2.0 %copy-start.2 = (s32[3,512]{1,0:T(4,128)S(1)}, s32[3,512]{1,0:T(4,128)}, u32[]{:S(2)}) copy-start(s32[3,512]{1,0:T(4,128)} %param.7) | copy-start | bytes 18436
Sparse Core Ops, SparseCore 0:
  22.9 66.6 reduce-scatter.3
where the time goes:
time: 165 us
  waiting for transfers between devices  66.8 us (40%)
  blocking collectives  45 us (27%)
  matrix products  22.1 us (13%)
  local copies, waits for them, and re-layouts  15.9 us (10%)
  between operations  13.6 us (8%)
    unnamed x2, waiting for transfers between devices  66.8 us
    all_gather x1, blocking collectives, per_device(): fragment = lax.all_gather(reduced, 'ka', axis=1, tiled=True)  23.7 us
    all_to_all x1, blocking collectives, per_device(): lax.all_to_all(combined, 'rp', split_axis=0, concat_axis=2, tiled=True)  21.3 us
    dot_general x1, matrix products, per_device(): jnp.dot(sin_part, fragment[1], precision=high, preferred_element_type=jnp...  4.75 us
    dot_general x1, matrix products, per_device(): jnp.dot(sin_part, fragment[0], precision=high, preferred_element_type=jnp...  4.53 us
    dot_general x1, matrix products, per_device(): jnp.dot(cos_part, fragment[1], precision=high, preferred_element_type=jnp...  4.5 us
    dot_general x1, matrix products, per_device(): jnp.dot(cos_part, fragment[0], precision=high, preferred_element_type=jnp...  4.49 us
    slice x1, local copies, waits for them, and re-layouts, per_device(): imag_in = values[:, :, 1, :]  4.48 us
  transfers between devices with their start and end apart: 1, of which 1 were waited for; matrix products, arithmetic and copies ran while one was open for 0% of the time, Pallas kernels for 0%

commit v1 on v0

v1 whole, which is shorter than its diff:
```python
import functools
import math

import jax
import jax.numpy as jnp
from jax import lax
from jax.experimental import pallas as pl
from jax.experimental.pallas import tpu as pltpu
from jax.sharding import PartitionSpec as P

NKG = 16
LANES = 128
HALF = 64
QUARTER = [math.cos(2.0 * math.pi * n / NKG) for n in range(4)] + [0.0]


def cosine(n):
    m = n & (NKG - 1)
    t = jnp.minimum(m, NKG - m)
    u = jnp.minimum(t, 8 - t)
    value = jnp.full(n.shape, QUARTER[0], jnp.float32)
    for i in range(1, 5):
        value = jnp.where(u == i, jnp.float32(QUARTER[i]), value)
    return jnp.where(t > 4, -value, value)


def wave_sums(q_ref, rp_ref, table_ref, out_ref, weights_ref):
    groups = weights_ref.shape[1] // 16

    @pl.when(pl.program_id(0) == 0)
    def _():
        lane = lax.broadcasted_iota(jnp.int32, (16, 256), 1)
        row = lax.broadcasted_iota(jnp.int32, (16, 256), 0)
        spread = jnp.where((lane & 15) == row, 1.0, 0.0).astype(jnp.bfloat16)
        vectors = jnp.dot(
            rp_ref[...].astype(jnp.float32).astype(jnp.bfloat16),
            spread,
            preferred_element_type=jnp.float32,
        ).astype(jnp.int32)
        own = (lane >> 4) == row
        for q in range(2):
            n = (
                q_ref[0, q] * vectors[0:1]
                + q_ref[1, q] * vectors[1:2]
                + q_ref[2, q] * vectors[2:3]
            )
            for part, value in enumerate((cosine(n), cosine(n - 4))):
                high = value.astype(jnp.bfloat16).astype(jnp.float32)
                for fine, piece in enumerate((high, value - high)):
                    at = 64 * fine + 32 * part + 16 * q
                    block = jnp.where(own, jnp.broadcast_to(piece, (16, 256)), 0.0)
                    weights_ref[at : at + 16, :] = block.astype(jnp.bfloat16)

    y = jnp.dot(weights_ref[...], table_ref[...], preferred_element_type=jnp.float32)
    y = y[:64] + y[64:]
    by_cos, by_sin = y[:32], y[32:]
    real = by_cos[:, :512] - by_sin[:, 512:]
    imag = by_sin[:, :512] + by_cos[:, 512:]
    low = lax.broadcasted_iota(jnp.int32, (16, LANES), 1) < HALF
    for q in range(2):
        for b in range(4):
            re = real[16 * q : 16 * q + 16, LANES * b : LANES * (b + 1)]
            im = imag[16 * q : 16 * q + 16, LANES * b : LANES * (b + 1)]
            first = jnp.where(low, re, pltpu.roll(im, HALF, 1))
            second = jnp.where(low, pltpu.roll(re, HALF, 1), im)
            out_ref[8 * q + 2 * b] = first.astype(out_ref.dtype)
            out_ref[8 * q + 2 * b + 1] = second.astype(out_ref.dtype)


def add_parts(parts_ref, out_ref):
    total = parts_ref[0].astype(jnp.float32)
    for r in range(1, parts_ref.shape[0]):
        total = total + parts_ref[r].astype(jnp.float32)
    high = total.astype(jnp.bfloat16)
    low = (total - high.astype(jnp.float32)).astype(jnp.bfloat16)
    for a in range(out_ref.shape[0]):
        out_ref[a, 0] = high
        out_ref[a, 1] = low


def bloch(mid_ref, k_ref, re_ref, out_ref, phase_ref):
    k = k_ref[...].astype(jnp.float32).astype(jnp.bfloat16)
    re = re_ref[...].astype(jnp.float32).astype(jnp.bfloat16)
    n = lax.dot_general(k, re, (((0,), (0,)), ((), ())), preferred_element_type=jnp.float32)
    n = n.astype(jnp.int32)
    phase_ref[:, :512] = cosine(n).astype(jnp.bfloat16)
    phase_ref[:, 512:] = cosine(n - 4).astype(jnp.bfloat16)
    low = lax.broadcasted_iota(jnp.int32, (512, LANES), 1) < HALF
    straight, turned = [], []
    for piece in range(2):
        x = mid_ref[:, piece].reshape(512, LANES).astype(jnp.float32)
        rolled = pltpu.roll(x, HALF, 1)
        straight.append(x)
        turned.append(jnp.where(low, -rolled, rolled))
    with_cos = jnp.concatenate(straight, axis=1).astype(jnp.bfloat16)
    with_sin = jnp.concatenate(turned, axis=1).astype(jnp.bfloat16)
    out = jnp.dot(phase_ref[:, :512], with_cos, preferred_element_type=jnp.float32)
    out = out + jnp.dot(phase_ref[:, 512:], with_sin, preferred_element_type=jnp.float32)
    out_ref[...] = out[:, :LANES] + out[:, LANES:]


def place(pieces_ref, out_ref):
    low = lax.broadcasted_iota(jnp.int32, (32, LANES), 1) < HALF
    for pair in range(8):
        x0 = pieces_ref[2 * pair].astype(jnp.float32)
        x1 = pieces_ref[2 * pair + 1].astype(jnp.float32)
        at = LANES * pair
        out_ref[:, at : at + LANES] = jnp.where(low, x0, pltpu.roll(x1, HALF, 1))
        out_ref[:, 1024 + at : 1024 + at + LANES] = jnp.where(low, pltpu.roll(x0, HALF, 1), x1)


def per_device(coupling_table, k_points, re_vectors, rp_vectors, q_points):
    vmem = pl.BlockSpec(memory_space=pltpu.VMEM)
    smem = pl.BlockSpec(memory_space=pltpu.SMEM)
    table = coupling_table.reshape(1024, 1024)
    parts = pl.pallas_call(
        wave_sums,
        grid=(4,),
        in_specs=[smem, vmem, pl.BlockSpec((256, 1024), lambda g: (g, 0))],
        out_specs=pl.BlockSpec((16, 16, LANES), lambda g: (0, g, 0)),
        out_shape=jax.ShapeDtypeStruct((16, 64, LANES), jnp.bfloat16),
        scratch_shapes=[pltpu.VMEM((128, 256), jnp.bfloat16)],
        name="wave_sums",
    )(q_points, rp_vectors, table)
    parts = lax.all_to_all(parts, "rp", 0, 0, tiled=True)
    mid = pl.pallas_call(
        add_parts,
        in_specs=[vmem],
        out_specs=vmem,
        out_shape=jax.ShapeDtypeStruct((8, 2, 64, LANES), jnp.bfloat16),
        name="add_parts",
    )(parts)
    mid = lax.all_to_all(mid, "ka", 0, 0, tiled=True)
    columns = pl.pallas_call(
        bloch,
        in_specs=[vmem, vmem, vmem],
        out_specs=vmem,
        out_shape=jax.ShapeDtypeStruct((512, LANES), jnp.float32),
        scratch_shapes=[pltpu.VMEM((512, 1024), jnp.bfloat16)],
        name="bloch",
    )(mid, k_points, re_vectors)
    pieces = lax.all_to_all(columns.reshape(16, 32, LANES), "rp", 0, 0, tiled=True)
    return pl.pallas_call(
        place,
        in_specs=[vmem],
        out_specs=vmem,
        out_shape=jax.ShapeDtypeStruct((32, 2048), jnp.float32),
        name="place",
    )(pieces)


def solution(mesh):
    placed = (P("ka", "rp", None), P(None, "ka"), P(), P(None, "rp"), P())
    return jax.shard_map(
        per_device, mesh=mesh, in_specs=placed, out_specs=P(("ka", "rp"), None), check_vma=False
    )
```

time: 165 us -> 56.6 us (0.34)
  waiting for transfers between devices: 66.8 us -> 0 us
  matrix products: 22.1 us -> 0 us
  local copies, waits for them, and re-layouts: 15.9 us -> 1.35 us
  between operations: 13.6 us -> 0.01 us
  Pallas kernels: 0 us -> 11.1 us
    unnamed x2 -> x0, waiting for transfers between devices: 66.8 us -> none
    all_gather x1 -> x0, blocking collectives: 23.7 us -> none  [per_device(): fragment = lax.all_gather(reduced, 'ka', axis=1, tiled=True)]
    all_to_all x1 -> x3, blocking collectives: 21.3 us -> 43.6 us  [the longest x1 17.9 us: per_device(): parts = lax.all_to_all(parts, 'rp', 0, 0, tiled=True)]
    dot_general x8 -> x0, matrix products: 22.1 us -> none  [the longest x1 4.75 us: per_device(): jnp.dot(sin_part, fragment[1], precision=high, preferred_element_type=jnp...]
    pallas_call x0 -> x4, Pallas kernels: none -> 11.1 us  [the longest x1 4.19 us: per_device(): pl.pallas_call(wave_sums, grid=(4,), in_specs=[smem, vmem, pl.BlockSpec((...]
    slice x4 -> x0, local copies, waits for them, and re-layouts: 5.5 us -> none  [the longest x1 4.48 us: per_device(): imag_in = values[:, :, 1, :]]
    reshape x2 -> x0, local copies, waits for them, and re-layouts: 4.2 us -> none  [the longest x1 3.32 us: per_device(): coupling_table.astype(jnp.float32).reshape(local_re, local_rp, 2, entries)]
    unnamed x12 -> x1, local copies, waits for them, and re-layouts: 3.87 us -> 1.35 us
  transfers between devices with their start and end apart: 1 -> 0, of which waited for: 1 -> 0; matrix products, arithmetic and copies ran while one was open for 0% -> 0% of each run, Pallas kernels for 0% -> 0%
where the time goes in v1:
time: 56.6 us; the launch traced here: 56 us
  blocking collectives  43.6 us (77%)
  Pallas kernels  11.1 us (20%)
  local copies, waits for them, and re-layouts  1.35 us (2%)
    all_to_all x1, blocking collectives, per_device(): parts = lax.all_to_all(parts, 'rp', 0, 0, tiled=True)  17.9 us
    all_to_all x1, blocking collectives, per_device(): lax.all_to_all(columns.reshape(16, 32, LANES), 'rp', 0, 0, tiled=True)  15.1 us
    all_to_all x1, blocking collectives, per_device(): mid = lax.all_to_all(mid, 'ka', 0, 0, tiled=True)  10.6 us
    pallas_call x1, Pallas kernels, per_device(): pl.pallas_call(wave_sums, grid=(4,), in_specs=[smem, vmem, pl.BlockSpec((...  4.19 us
    pallas_call x1, Pallas kernels, per_device(): pl.pallas_call(bloch, in_specs=[vmem, vmem, vmem], out_specs=vmem, out_sh...  3.41 us
    pallas_call x1, Pallas kernels, per_device(): pl.pallas_call(place, in_specs=[vmem], out_specs=vmem, out_shape=jax.Shap...  1.79 us
    pallas_call x1, Pallas kernels, per_device(): pl.pallas_call(add_parts, in_specs=[vmem], out_specs=vmem, out_shape=jax....  1.7 us
    unnamed x1, local copies, waits for them, and re-layouts  1.35 us

profile of v1, /device:TPU:1, one launch (start us, length us, event | category | flops | bytes accessed | tf_op | source)
XLA Modules:
  0.0 56.0 jit_solution(9816649380586775796)
XLA Ops:
  0.0 1.4 %copy.6.q_ref = s32[3,2]{1,0:T(4,128)} copy(s32[3,2]{0,1:T(2,128)} %param.9) | data formatting | bytes 48 | tf_op args[4]
  1.4 4.2 %wave_sums.1 = bf16[16,64,128]{2,1,0:T(8,128)(2,1)} custom-call(s32[3,2]{1,0:T(4,128)} %copy.6.q_ref, s32[3,16]{1,0:T(4,128)} %rp_ref.1, bf16[1024,1024]{1,0:T(8,128)(2,1)} %bitcast.2), custom_call_target="tpu_custom_call" | custom-call | tf_op jit(solution)/shard_map/wave_sums/pallas_call | solution.py:116
  5.5 17.9 %all_to_all.15.parts_ref = bf16[16,64,128]{2,1,0:T(8,128)(2,1)} all-to-all(bf16[16,64,128]{2,1,0:T(8,128)(2,1)} %wave_sums.1), channel_id=1, replica_groups=mesh['ka'=8,'rp'=16] {'rp'}, dimensions={0} | all-to-all | bytes 524288 | tf_op jit(solution)/shard_map/all_to_all | solution.py:125
  23.5 1.7 %add_parts.1 = bf16[8,2,64,128]{3,2,1,0:T(8,128)(2,1)} custom-call(bf16[16,64,128]{2,1,0:T(8,128)(2,1)} %all_to_all.15.parts_ref), custom_call_target="tpu_custom_call" | custom-call | tf_op jit(solution)/shard_map/add_parts/pallas_call | solution.py:126
  25.2 10.6 %all_to_all.16.mid_ref = bf16[8,2,64,128]{3,2,1,0:T(8,128)(2,1)} all-to-all(bf16[8,2,64,128]{3,2,1,0:T(8,128)(2,1)} %add_parts.1), channel_id=1, replica_groups=mesh['ka'=8,'rp'=16] {'ka'}, dimensions={0} | all-to-all | bytes 524288 | tf_op jit(solution)/shard_map/all_to_all | solution.py:133
  35.7 3.4 %bloch.1 = f32[512,128]{1,0:T(8,128)} custom-call(bf16[8,2,64,128]{3,2,1,0:T(8,128)(2,1)} %all_to_all.16.mid_ref, s32[3,512]{1,0:T(4,128)} %k_ref.1, s32[3,512]{1,0:T(4,128)} %re_ref.1), custom_call_target="tpu_custom_call" | custom-call | tf_op jit(solution)/shard_map/bloch/pallas_call | solution.py:134
  39.1 15.1 %all_to_all.17.pieces_ref = f32[16,32,128]{2,1,0:T(8,128)} all-to-all(f32[16,32,128]{2,1,0:T(8,128)} %bitcast.3), channel_id=1, replica_groups=mesh['ka'=8,'rp'=16] {'rp'}, dimensions={0} | all-to-all | bytes 524288 | tf_op jit(solution)/shard_map/all_to_all | solution.py:142
  54.2 1.8 %place.1 = f32[32,2048]{1,0:T(8,128)} custom-call(f32[16,32,128]{2,1,0:T(8,128)} %all_to_all.17.pieces_ref), custom_call_target="tpu_custom_call" | custom-call | tf_op jit(solution)/shard_map/place/pallas_call | solution.py:143

commit v2 on v1

--- a/solution.py
+++ b/solution.py
@@ -40,9 +40,9 @@
         own = (lane >> 4) == row
         for q in range(2):
             n = (
-                q_ref[0, q] * vectors[0:1]
-                + q_ref[1, q] * vectors[1:2]
-                + q_ref[2, q] * vectors[2:3]
+                q_ref[q, 0] * vectors[0:1]
+                + q_ref[q, 1] * vectors[1:2]
+                + q_ref[q, 2] * vectors[2:3]
             )
             for part, value in enumerate((cosine(n), cosine(n - 4))):
                 high = value.astype(jnp.bfloat16).astype(jnp.float32)
@@ -109,6 +109,11 @@
         out_ref[:, 1024 + at : 1024 + at + LANES] = jnp.where(low, pltpu.roll(x0, HALF, 1), x1)
 
 
+def exchanged(x, axis):
+    x = lax.all_to_all(x, axis, 0, 0, tiled=True)
+    return pltpu.with_memory_space_constraint(x, pltpu.VMEM)
+
+
 def per_device(coupling_table, k_points, re_vectors, rp_vectors, q_points):
     vmem = pl.BlockSpec(memory_space=pltpu.VMEM)
     smem = pl.BlockSpec(memory_space=pltpu.SMEM)
@@ -118,28 +123,28 @@
         grid=(4,),
         in_specs=[smem, vmem, pl.BlockSpec((256, 1024), lambda g: (g, 0))],
         out_specs=pl.BlockSpec((16, 16, LANES), lambda g: (0, g, 0)),
-        out_shape=jax.ShapeDtypeStruct((16, 64, LANES), jnp.bfloat16),
+        out_shape=pltpu.VMEM((16, 64, LANES), jnp.bfloat16),
         scratch_shapes=[pltpu.VMEM((128, 256), jnp.bfloat16)],
         name="wave_sums",
-    )(q_points, rp_vectors, table)
-    parts = lax.all_to_all(parts, "rp", 0, 0, tiled=True)
+    )(q_points.T, rp_vectors, table)
+    parts = exchanged(parts, "rp")
     mid = pl.pallas_call(
         add_parts,
         in_specs=[vmem],
         out_specs=vmem,
-        out_shape=jax.ShapeDtypeStruct((8, 2, 64, LANES), jnp.bfloat16),
+        out_shape=pltpu.VMEM((8, 2, 64, LANES), jnp.bfloat16),
         name="add_parts",
     )(parts)
-    mid = lax.all_to_all(mid, "ka", 0, 0, tiled=True)
+    mid = exchanged(mid, "ka")
     columns = pl.pallas_call(
         bloch,
         in_specs=[vmem, vmem, vmem],
         out_specs=vmem,
-        out_shape=jax.ShapeDtypeStruct((512, LANES), jnp.float32),
+        out_shape=pltpu.VMEM((512, LANES), jnp.float32),
         scratch_shapes=[pltpu.VMEM((512, 1024), jnp.bfloat16)],
         name="bloch",
     )(mid, k_points, re_vectors)
-    pieces = lax.all_to_all(columns.reshape(16, 32, LANES), "rp", 0, 0, tiled=True)
+    pieces = exchanged(columns.reshape(16, 32, LANES), "rp")
     return pl.pallas_call(
         place,
         in_specs=[vmem],

time: 56.6 us -> 49 us (0.87)
  Pallas kernels: 11.1 us -> 6.65 us
  blocking collectives: 43.6 us -> 42 us
  local copies, waits for them, and re-layouts: 1.35 us -> 0 us
    pallas_call x1, Pallas kernels: 1.7 us -> 0.05 us  [per_device(): pl.pallas_call(add_parts, in_specs=[vmem], out_specs=vmem, out_shape=pltp...]
    all_to_all x3, blocking collectives: 43.6 us -> 42 us  [exchanged(): x = lax.all_to_all(x, axis, 0, 0, tiled=True)]
    unnamed x1 -> x0, local copies, waits for them, and re-layouts: 1.35 us -> none
    pallas_call x1, Pallas kernels: 3.41 us -> 2.44 us  [per_device(): pl.pallas_call(bloch, in_specs=[vmem, vmem, vmem], out_specs=vmem, out_sh...]
    pallas_call x1, Pallas kernels: 1.79 us -> 0.84 us  [per_device(): pl.pallas_call(place, in_specs=[vmem], out_specs=vmem, out_shape=jax.Shap...]
    pallas_call x1, Pallas kernels: 4.19 us -> 3.33 us  [per_device(): pl.pallas_call(wave_sums, grid=(4,), in_specs=[smem, vmem, pl.BlockSpec((...]
where the time goes in v2:
time: 49 us; the launch traced here: 48.7 us
  blocking collectives  42 us (86%)
  Pallas kernels  6.65 us (14%)
    all_to_all x3, blocking collectives, exchanged(): x = lax.all_to_all(x, axis, 0, 0, tiled=True)  42 us
    pallas_call x1, Pallas kernels, per_device(): pl.pallas_call(wave_sums, grid=(4,), in_specs=[smem, vmem, pl.BlockSpec((...  3.33 us
    pallas_call x1, Pallas kernels, per_device(): pl.pallas_call(bloch, in_specs=[vmem, vmem, vmem], out_specs=vmem, out_sh...  2.44 us

profile of v2, /device:TPU:1, one launch (start us, length us, event | category | flops | bytes accessed | tf_op | source)
XLA Modules:
  0.0 48.7 jit_solution(6027195329257623922)
XLA Ops:
  0.0 3.3 %wave_sums.1 = bf16[16,64,128]{2,1,0:T(8,128)(2,1)S(1)} custom-call(s32[2,3]{1,0:T(2,128)} %bitcast.5, s32[3,16]{1,0:T(4,128)} %rp_ref.1, bf16[1024,1024]{1,0:T(8,128)(2,1)} %bitcast.4), custom_call_target="tpu_custom_call" | custom-call | tf_op jit(solution)/shard_map/wave_sums/pallas_call | solution.py:121
  3.3 17.6 %all_to_all.15.parts_ref = bf16[16,64,128]{2,1,0:T(8,128)(2,1)S(1)} all-to-all(bf16[16,64,128]{2,1,0:T(8,128)(2,1)S(1)} %wave_sums.1), channel_id=1, replica_groups=mesh['ka'=8,'rp'=16] {'rp'}, dimensions={0} | all-to-all | bytes 524288 | tf_op jit(solution)/shard_map/all_to_all | solution.py:113
  21.0 10.3 %all_to_all.16.mid_ref = bf16[8,2,64,128]{3,2,1,0:T(8,128)(2,1)S(1)} all-to-all(bf16[8,2,64,128]{3,2,1,0:T(8,128)(2,1)S(1)} %add_parts.1), channel_id=1, replica_groups=mesh['ka'=8,'rp'=16] {'ka'}, dimensions={0} | all-to-all | bytes 524288 | tf_op jit(solution)/shard_map/all_to_all | solution.py:113
  31.2 2.4 %bloch.1 = f32[512,128]{1,0:T(8,128)S(1)} custom-call(bf16[8,2,64,128]{3,2,1,0:T(8,128)(2,1)S(1)} %all_to_all.16.mid_ref, s32[3,512]{1,0:T(4,128)} %k_ref.1, s32[3,512]{1,0:T(4,128)} %re_ref.1), custom_call_target="tpu_custom_call" | custom-call | tf_op jit(solution)/shard_map/bloch/pallas_call | solution.py:139
  33.7 14.2 %all_to_all.17.pieces_ref = f32[16,32,128]{2,1,0:T(8,128)S(1)} all-to-all(f32[16,32,128]{2,1,0:T(8,128)S(1)} %bitcast.3), channel_id=1, replica_groups=mesh['ka'=8,'rp'=16] {'rp'}, dimensions={0} | all-to-all | bytes 524288 | tf_op jit(solution)/shard_map/all_to_all | solution.py:113
  47.9 0.8 %place.1 = f32[32,2048]{1,0:T(8,128)} custom-call(f32[16,32,128]{2,1,0:T(8,128)S(1)} %all_to_all.17.pieces_ref), custom_call_target="tpu_custom_call" | custom-call | tf_op jit(solution)/shard_map/place/pallas_call | solution.py:148
  (1 shorter events, 0.0 us)

commit v3 on v1

v3 whole, which is shorter than its diff:
```python
import math

import jax
import jax.numpy as jnp
from jax import lax
from jax.experimental import pallas as pl
from jax.experimental.pallas import tpu as pltpu
from jax.sharding import PartitionSpec as P

NKG = 16
LANES = 128
HALF = 64
CHUNKS = 4
ROWS = 1024 // CHUNKS
QUARTER = [math.cos(2.0 * math.pi * n / NKG) for n in range(4)] + [0.0]
BITS = 14
SMALLEST = 2.0**-100


def cosine(n):
    m = n & (NKG - 1)
    t = jnp.minimum(m, NKG - m)
    u = jnp.minimum(t, 8 - t)
    value = jnp.full(n.shape, QUARTER[0], jnp.float32)
    for i in range(1, 5):
        value = jnp.where(u == i, jnp.float32(QUARTER[i]), value)
    return jnp.where(t > 4, -value, value)


def lower_half(rows):
    return lax.broadcasted_iota(jnp.int32, (rows, LANES), 1) < HALF


def exact(x):
    return x.astype(jnp.float32).astype(jnp.bfloat16)


def pack(x):
    most = jnp.maximum(jnp.max(jnp.abs(x), axis=0, keepdims=True), SMALLEST)
    exponent = jnp.ceil(jnp.log2(most))
    packed = jnp.round(x * jnp.exp2(BITS - exponent)).astype(jnp.int32).astype(jnp.int16)
    header = jnp.broadcast_to(exponent, (8, LANES)).astype(jnp.int32).astype(jnp.int16)
    return packed, header


def unpack(block):
    rows = block.shape[0] - 8
    exponent = block[rows:].astype(jnp.int32).astype(jnp.float32)
    unit = jnp.exp2(exponent - BITS)[0:1]
    return block[:rows].astype(jnp.int32).astype(jnp.float32) * unit


def fill_weights(q_ref, rp_ref, weights_ref):
    lane = lax.broadcasted_iota(jnp.int32, (16, 256), 1)
    row = lax.broadcasted_iota(jnp.int32, (16, 256), 0)
    spread = jnp.where((lane & 15) == row, 1.0, 0.0).astype(jnp.bfloat16)
    vectors = jnp.dot(exact(rp_ref[...]), spread, preferred_element_type=jnp.float32).astype(jnp.int32)
    own = (lane >> 4) == row
    for q in range(2):
        n = sum(q_ref[q, d] * vectors[d : d + 1] for d in range(3))
        for part, value in enumerate((cosine(n), cosine(n - 4))):
            high = value.astype(jnp.bfloat16).astype(jnp.float32)
            for fine, piece in enumerate((high, value - high)):
                at = 64 * fine + 32 * part + 16 * q
                block = jnp.where(own, jnp.broadcast_to(piece, (16, 256)), 0.0)
                weights_ref[at : at + 16, :] = block.astype(jnp.bfloat16)


def fill_phases(k_ref, re_ref, phase_ref):
    n = lax.dot_general(
        exact(k_ref[...]), exact(re_ref[...]), (((0,), (0,)), ((), ())), preferred_element_type=jnp.float32
    )
    n = n.astype(jnp.int32) & (NKG - 1)
    lane = lax.broadcasted_iota(jnp.int32, (8, LANES), 1)
    tables = [jnp.broadcast_to(cosine(lane - turn)[0:1], (512, LANES)) for turn in (0, 4)]
    for b in range(4):
        index = n[:, LANES * b : LANES * (b + 1)]
        for i, table in enumerate(tables):
            at = 512 * i + LANES * b
            phase_ref[:, at : at + LANES] = jnp.take_along_axis(table, index, axis=1).astype(jnp.bfloat16)


def wave_sums(table_hbm, k_hbm, re_hbm, rp_hbm, q_hbm, out_ref, phase_ref, table, k, re, rp, q, weights, sems):
    copies = [
        pltpu.make_async_copy(source, target, sems.at[CHUNKS + i])
        for i, (source, target) in enumerate(((k_hbm, k), (re_hbm, re), (rp_hbm, rp), (q_hbm, q)))
    ]
    chunks = [
        pltpu.make_async_copy(
            table_hbm.at[ROWS * g : ROWS * (g + 1)], table.at[ROWS * g : ROWS * (g + 1)], sems.at[g]
        )
        for g in range(CHUNKS)
    ]
    for copy in copies + chunks:
        copy.start()
    for copy in copies:
        copy.wait()
    fill_weights(q, rp, weights)
    fill_phases(k, re, phase_ref)
    low = lower_half(16)
    for g in range(CHUNKS):
        chunks[g].wait()
        y = jnp.dot(weights[...], table[ROWS * g : ROWS * (g + 1)], preferred_element_type=jnp.float32)
        y = y[:64] + y[64:]
        by_cos, by_sin = y[:32], y[32:]
        real = by_cos[:, :512] - by_sin[:, 512:]
        imag = by_sin[:, :512] + by_cos[:, 512:]
        rows = slice(16 * g, 16 * g + 16)
        for w in range(2):
            for b in range(4):
                re_part = real[16 * w : 16 * w + 16, LANES * b : LANES * (b + 1)]
                im_part = imag[16 * w : 16 * w + 16, LANES * b : LANES * (b + 1)]
                first = jnp.where(low, re_part, pltpu.roll(im_part, HALF, 1))
                second = jnp.where(low, pltpu.roll(re_part, HALF, 1), im_part)
                out_ref[8 * w + 2 * b, rows] = first.astype(out_ref.dtype)
                out_ref[8 * w + 2 * b + 1, rows] = second.astype(out_ref.dtype)


def add_parts(parts_ref, out_ref):
    total = parts_ref[0].astype(jnp.float32)
    for r in range(1, 16):
        total = total + parts_ref[r].astype(jnp.float32)
    packed, header = pack(total)
    for a in range(8):
        out_ref[a, :64] = packed
        out_ref[a, 64:] = header


def bloch(mid_ref, phase_ref, out_ref):
    straight, turned = [], []
    low = lower_half(64)
    for a in range(8):
        x = unpack(mid_ref[a])
        high = x.astype(jnp.bfloat16).astype(jnp.float32)
        row, turned_row = [], []
        for piece in (high, x - high):
            rolled = pltpu.roll(piece, HALF, 1)
            row.append(piece)
            turned_row.append(jnp.where(low, -rolled, rolled))
        straight.append(jnp.concatenate(row, axis=1).astype(jnp.bfloat16))
        turned.append(jnp.concatenate(turned_row, axis=1).astype(jnp.bfloat16))
    both = jnp.concatenate(straight + turned, axis=0)
    out = jnp.dot(phase_ref[...], both, preferred_element_type=jnp.float32)
    packed, header = pack(out[:, :LANES] + out[:, LANES:])
    for r in range(16):
        out_ref[r, :32] = packed[32 * r : 32 * r + 32]
        out_ref[r, 32:] = header


def place(pieces_ref, out_ref):
    low = lower_half(32)
    for pair in range(8):
        x0 = unpack(pieces_ref[2 * pair])
        x1 = unpack(pieces_ref[2 * pair + 1])
        at = LANES * pair
        out_ref[:, at : at + LANES] = jnp.where(low, x0, pltpu.roll(x1, HALF, 1))
        out_ref[:, 1024 + at : 1024 + at + LANES] = jnp.where(low, pltpu.roll(x0, HALF, 1), x1)


def in_vmem(x):
    return pltpu.with_memory_space_constraint(x, pltpu.VMEM)


def per_device(coupling_table, k_points, re_vectors, rp_vectors, q_points):
    vmem = pl.BlockSpec(memory_space=pltpu.VMEM)
    parts, phase = pl.pallas_call(
        wave_sums,
        in_specs=[pl.BlockSpec(memory_space=pl.ANY)] * 5,
        out_specs=[vmem, vmem],
        out_shape=[pltpu.VMEM((16, 64, LANES), jnp.bfloat16), pltpu.VMEM((512, 1024), jnp.bfloat16)],
        scratch_shapes=[
            pltpu.VMEM((1024, 1024), jnp.bfloat16),
            pltpu.VMEM((3, 512), jnp.int32),
            pltpu.VMEM((3, 512), jnp.int32),
            pltpu.VMEM((3, 16), jnp.int32),
            pltpu.SMEM((2, 3), jnp.int32),
            pltpu.VMEM((128, 256), jnp.bfloat16),
            pltpu.SemaphoreType.DMA((CHUNKS + 4,)),
        ],
        name="wave_sums",
    )(coupling_table.reshape(1024, 1024), k_points, re_vectors, rp_vectors, q_points.T)
    parts = lax.all_to_all(parts, "rp", 0, 0, tiled=True)
    mid = pl.pallas_call(
        add_parts,
        in_specs=[vmem],
        out_specs=vmem,
        out_shape=pltpu.VMEM((8, 72, LANES), jnp.int16),
        name="add_parts",
    )(in_vmem(parts))
    mid = lax.all_to_all(mid, "ka", 0, 0, tiled=True)
    pieces = pl.pallas_call(
        bloch,
        in_specs=[vmem, vmem],
        out_specs=vmem,
        out_shape=pltpu.VMEM((16, 40, LANES), jnp.int16),
        name="bloch",
    )(in_vmem(mid), in_vmem(phase))
    pieces = lax.all_to_all(pieces, "rp", 0, 0, tiled=True)
    return pl.pallas_call(
        place,
        in_specs=[vmem],
        out_specs=vmem,
        out_shape=jax.ShapeDtypeStruct((32, 2048), jnp.float32),
        name="place",
    )(in_vmem(pieces))


def solution(mesh):
    placed = (P("ka", "rp", None), P(None, "ka"), P(), P(None, "rp"), P())
    return jax.shard_map(
        per_device, mesh=mesh, in_specs=placed, out_specs=P(("ka", "rp"), None), check_vma=False
    )
```

time: 56.6 us -> 45.4 us (0.80)
  Pallas kernels: 11.1 us -> 4.63 us
  blocking collectives: 43.6 us -> 40.5 us
  local copies, waits for them, and re-layouts: 1.35 us -> 0 us
    pallas_call x3, Pallas kernels: 9.3 us -> 3.79 us  [the longest x1 3.13 us: per_device(): pl.pallas_call(wave_sums, in_specs=[pl.BlockSpec(memory_space=pl.ANY)] *...]
    all_to_all x1, blocking collectives: 15.1 us -> 13.1 us  [per_device(): pieces = lax.all_to_all(pieces, 'rp', 0, 0, tiled=True)]
    unnamed x1 -> x0, local copies, waits for them, and re-layouts: 1.35 us -> none
    pallas_call x1, Pallas kernels: 1.79 us -> 0.85 us  [per_device(): pl.pallas_call(place, in_specs=[vmem], out_specs=vmem, out_shape=jax.Shap...]
    all_to_all x1, blocking collectives: 10.6 us -> 9.78 us  [per_device(): mid = lax.all_to_all(mid, 'ka', 0, 0, tiled=True)]
where the time goes in v3:
time: 45.4 us; the launch traced here: 45.1 us
  blocking collectives  40.5 us (89%)
  Pallas kernels  4.63 us (10%)
    all_to_all x1, blocking collectives, per_device(): parts = lax.all_to_all(parts, 'rp', 0, 0, tiled=True)  17.6 us
    all_to_all x1, blocking collectives, per_device(): pieces = lax.all_to_all(pieces, 'rp', 0, 0, tiled=True)  13.1 us
    all_to_all x1, blocking collectives, per_device(): mid = lax.all_to_all(mid, 'ka', 0, 0, tiled=True)  9.78 us
    pallas_call x1, Pallas kernels, per_device(): pl.pallas_call(wave_sums, in_specs=[pl.BlockSpec(memory_space=pl.ANY)] *...  3.13 us

profile of v3, /device:TPU:1, one launch (start us, length us, event | category | flops | bytes accessed | tf_op | source)
XLA Modules:
  0.0 45.1 jit_solution(2494313343287419662)
XLA Ops:
  0.0 3.1 %wave_sums.1 = (bf16[16,64,128]{2,1,0:T(8,128)(2,1)S(1)}, bf16[512,1024]{1,0:T(8,128)(2,1)S(1)}) custom-call(bf16[1024,1024]{1,0:T(8,128)(2,1)} %bitcast.2, s32[3,512]{1,0:T(4,128)} %k_hbm.1, s32[3,512]{1,0:T(4,128)} %re_hbm.1, s32[3,16]{1,0:T(4,128)} %rp_hbm.1, s32[2,3]{1,0:T(2,128)} %bitcast.3), custom_call_target="tpu_custom_call" | custom-call | tf_op jit(solution)/shard_map/wave_sums/pallas_call | solution.py:166
  3.1 17.6 %all_to_all.15.parts_ref = bf16[16,64,128]{2,1,0:T(8,128)(2,1)S(1)} all-to-all(bf16[16,64,128]{2,1,0:T(8,128)(2,1)S(1)} %get-tuple-element.7), channel_id=1, replica_groups=mesh['ka'=8,'rp'=16] {'rp'}, dimensions={0} | all-to-all | bytes 524288 | tf_op jit(solution)/shard_map/all_to_all | solution.py:182
  20.7 0.1 add_parts.1
  20.8 9.8 %all_to_all.16.mid_ref = s16[8,72,128]{2,1,0:T(8,128)(2,1)S(1)} all-to-all(s16[8,72,128]{2,1,0:T(8,128)(2,1)S(1)} %add_parts.1), channel_id=1, replica_groups=mesh['ka'=8,'rp'=16] {'ka'}, dimensions={0} | all-to-all | bytes 294912 | tf_op jit(solution)/shard_map/all_to_all | solution.py:190
  30.6 0.6 %bloch.1 = s16[16,40,128]{2,1,0:T(8,128)(2,1)S(1)} custom-call(s16[8,72,128]{2,1,0:T(8,128)(2,1)S(1)} %all_to_all.16.mid_ref, bf16[512,1024]{1,0:T(8,128)(2,1)S(1)} %get-tuple-element.8.phase_ref), custom_call_target="tpu_custom_call" | custom-call | tf_op jit(solution)/shard_map/bloch/pallas_call | solution.py:191
  31.2 13.1 %all_to_all.17.pieces_ref = s16[16,40,128]{2,1,0:T(8,128)(2,1)S(1)} all-to-all(s16[16,40,128]{2,1,0:T(8,128)(2,1)S(1)} %bloch.1), channel_id=1, replica_groups=mesh['ka'=8,'rp'=16] {'rp'}, dimensions={0} | all-to-all | bytes 327680 | tf_op jit(solution)/shard_map/all_to_all | solution.py:198
  44.3 0.8 %place.1 = f32[32,2048]{1,0:T(8,128)} custom-call(s16[16,40,128]{2,1,0:T(8,128)(2,1)S(1)} %all_to_all.17.pieces_ref), custom_call_target="tpu_custom_call" | custom-call | tf_op jit(solution)/shard_map/place/pallas_call | solution.py:199

commit v4 on v3

--- a/solution.py
+++ b/solution.py
@@ -10,7 +10,7 @@
 NKG = 16
 LANES = 128
 HALF = 64
-CHUNKS = 4
+CHUNKS = 1
 ROWS = 1024 // CHUNKS
 QUARTER = [math.cos(2.0 * math.pi * n / NKG) for n in range(4)] + [0.0]
 BITS = 14
@@ -80,10 +80,10 @@
             phase_ref[:, at : at + LANES] = jnp.take_along_axis(table, index, axis=1).astype(jnp.bfloat16)
 
 
-def wave_sums(table_hbm, k_hbm, re_hbm, rp_hbm, q_hbm, out_ref, phase_ref, table, k, re, rp, q, weights, sems):
-    copies = [
+def wave_sums(table_hbm, rp_hbm, q_hbm, keep_ref, send_ref, table, rp, q, weights, sems):
+    small = [
         pltpu.make_async_copy(source, target, sems.at[CHUNKS + i])
-        for i, (source, target) in enumerate(((k_hbm, k), (re_hbm, re), (rp_hbm, rp), (q_hbm, q)))
+        for i, (source, target) in enumerate(((rp_hbm, rp), (q_hbm, q)))
     ]
     chunks = [
         pltpu.make_async_copy(
@@ -91,16 +91,17 @@
         )
         for g in range(CHUNKS)
     ]
-    for copy in copies + chunks:
+    for copy in small + chunks:
         copy.start()
-    for copy in copies:
+    for copy in small:
         copy.wait()
     fill_weights(q, rp, weights)
-    fill_phases(k, re, phase_ref)
     low = lower_half(16)
-    for g in range(CHUNKS):
-        chunks[g].wait()
-        y = jnp.dot(weights[...], table[ROWS * g : ROWS * (g + 1)], preferred_element_type=jnp.float32)
+    core0 = (lax.axis_index("rp") & 1) == 0
+    for g in range(4):
+        if (256 * g) % ROWS == 0:
+            chunks[256 * g // ROWS].wait()
+        y = jnp.dot(weights[...], table[256 * g : 256 * (g + 1)], preferred_element_type=jnp.float32)
         y = y[:64] + y[64:]
         by_cos, by_sin = y[:32], y[32:]
         real = by_cos[:, :512] - by_sin[:, 512:]
@@ -108,17 +109,21 @@
         rows = slice(16 * g, 16 * g + 16)
         for w in range(2):
             for b in range(4):
-                re_part = real[16 * w : 16 * w + 16, LANES * b : LANES * (b + 1)]
-                im_part = imag[16 * w : 16 * w + 16, LANES * b : LANES * (b + 1)]
-                first = jnp.where(low, re_part, pltpu.roll(im_part, HALF, 1))
-                second = jnp.where(low, pltpu.roll(re_part, HALF, 1), im_part)
-                out_ref[8 * w + 2 * b, rows] = first.astype(out_ref.dtype)
-                out_ref[8 * w + 2 * b + 1, rows] = second.astype(out_ref.dtype)
+                re = real[16 * w : 16 * w + 16, LANES * b : LANES * (b + 1)]
+                im = imag[16 * w : 16 * w + 16, LANES * b : LANES * (b + 1)]
+                first = jnp.where(low, re, pltpu.roll(im, HALF, 1))
+                second = jnp.where(low, pltpu.roll(re, HALF, 1), im)
+                keep_ref[4 * w + b, rows] = jnp.where(core0, first, second)
+                send_ref[4 * w + b, rows] = jnp.where(core0, second, first)
+
+
+def add_cores(keep_ref, got_ref, out_ref):
+    out_ref[...] = (keep_ref[...] + got_ref[...]).astype(out_ref.dtype)
 
 
 def add_parts(parts_ref, out_ref):
     total = parts_ref[0].astype(jnp.float32)
-    for r in range(1, 16):
+    for r in range(1, 8):
         total = total + parts_ref[r].astype(jnp.float32)
     packed, header = pack(total)
     for a in range(8):
@@ -163,23 +168,38 @@
 
 def per_device(coupling_table, k_points, re_vectors, rp_vectors, q_points):
     vmem = pl.BlockSpec(memory_space=pltpu.VMEM)
-    parts, phase = pl.pallas_call(
+    same_core = [[2 * chip + core for chip in range(8)] for core in range(2)]
+    keep, send = pl.pallas_call(
         wave_sums,
-        in_specs=[pl.BlockSpec(memory_space=pl.ANY)] * 5,
+        in_specs=[pl.BlockSpec(memory_space=pl.ANY)] * 3,
         out_specs=[vmem, vmem],
-        out_shape=[pltpu.VMEM((16, 64, LANES), jnp.bfloat16), pltpu.VMEM((512, 1024), jnp.bfloat16)],
+        out_shape=[pltpu.VMEM((8, 64, LANES), jnp.float32)] * 2,
         scratch_shapes=[
             pltpu.VMEM((1024, 1024), jnp.bfloat16),
-            pltpu.VMEM((3, 512), jnp.int32),
-            pltpu.VMEM((3, 512), jnp.int32),
             pltpu.VMEM((3, 16), jnp.int32),
             pltpu.SMEM((2, 3), jnp.int32),
             pltpu.VMEM((128, 256), jnp.bfloat16),
-            pltpu.SemaphoreType.DMA((CHUNKS + 4,)),
+            pltpu.SemaphoreType.DMA((CHUNKS + 2,)),
         ],
         name="wave_sums",
-    )(coupling_table.reshape(1024, 1024), k_points, re_vectors, rp_vectors, q_points.T)
-    parts = lax.all_to_all(parts, "rp", 0, 0, tiled=True)
+    )(coupling_table.reshape(1024, 1024), rp_vectors, q_points.T)
+    got = lax.ppermute(send, "rp", [(i, i ^ 1) for i in range(16)])
+    phase = pl.pallas_call(
+        fill_phases,
+        in_specs=[vmem, vmem],
+        out_specs=vmem,
+        out_shape=pltpu.VMEM((512, 1024), jnp.bfloat16),
+        name="phases",
+    )(in_vmem(k_points), in_vmem(re_vectors))
+    got, phase = lax.optimization_barrier((got, phase))
+    parts = pl.pallas_call(
+        add_cores,
+        in_specs=[vmem, vmem],
+        out_specs=vmem,
+        out_shape=pltpu.VMEM((8, 64, LANES), jnp.bfloat16),
+        name="add_cores",
+    )(in_vmem(keep), in_vmem(got))
+    parts = lax.all_to_all(parts, "rp", 0, 0, axis_index_groups=same_core, tiled=True)
     mid = pl.pallas_call(
         add_parts,
         in_specs=[vmem],

time: 45.4 us -> 44.8 us (0.987)
  blocking collectives: 40.5 us -> 38.2 us
  starting transfers between devices: 0 us -> 1.5 us
    all_to_all x1, blocking collectives: 17.6 us -> 14.2 us  [per_device(): lax.all_to_all(parts, 'rp', 0, 0, axis_index_groups=same_core, tiled=True)]
    ppermute x0 -> x1, starting transfers between devices: none -> 1.5 us  [per_device(): got = lax.ppermute(send, 'rp', [(i, i ^ 1) for i in range(16)])]
    all_to_all x1, blocking collectives: 13.1 us -> 14.2 us  [per_device(): pieces = lax.all_to_all(pieces, 'rp', 0, 0, tiled=True)]
    pallas_call x0 -> x2, Pallas kernels: none -> 1.01 us  [the longest x1 0.98 us: per_device(): pl.pallas_call(fill_phases, in_specs=[vmem, vmem], out_specs=vmem, out_sh...]
    pallas_call x1, Pallas kernels: 3.13 us -> 2.2 us  [per_device(): pl.pallas_call(wave_sums, in_specs=[pl.BlockSpec(memory_space=pl.ANY)] *...]
  transfers between devices with their start and end apart: 0 -> 1, of which waited for: 0 -> 1; matrix products, arithmetic and copies ran while one was open for 0% -> 0% of each run, Pallas kernels for 0% -> 2%
where the time goes in v4:
time: 44.8 us; the launch traced here: 44.6 us
  blocking collectives  38.2 us (85%)
  Pallas kernels  4.69 us (10%)
  starting transfers between devices  1.5 us (3%)
    all_to_all x1, blocking collectives, per_device(): pieces = lax.all_to_all(pieces, 'rp', 0, 0, tiled=True)  14.2 us
    all_to_all x1, blocking collectives, per_device(): lax.all_to_all(parts, 'rp', 0, 0, axis_index_groups=same_core, tiled=True)  14.2 us
    all_to_all x1, blocking collectives, per_device(): mid = lax.all_to_all(mid, 'ka', 0, 0, tiled=True)  9.78 us
    pallas_call x1, Pallas kernels, per_device(): pl.pallas_call(wave_sums, in_specs=[pl.BlockSpec(memory_space=pl.ANY)] *...  2.2 us
    ppermute x1, starting transfers between devices, per_device(): got = lax.ppermute(send, 'rp', [(i, i ^ 1) for i in range(16)])  1.5 us
    pallas_call x1, Pallas kernels, per_device(): pl.pallas_call(fill_phases, in_specs=[vmem, vmem], out_specs=vmem, out_sh...  0.98 us
  transfers between devices with their start and end apart: 1, of which 1 were waited for; matrix products, arithmetic and copies ran while one was open for 0% of the time, Pallas kernels for 2%

profile of v4, /device:TPU:1, one launch (start us, length us, event | category | flops | bytes accessed | tf_op | source)
XLA Modules:
  0.0 44.6 jit_solution(10007243841081074216)
XLA Ops:
  0.0 0.0 copy-start.1
  0.0 0.0 copy-start
  0.0 2.2 %wave_sums.1 = (f32[8,64,128]{2,1,0:T(8,128)S(1)}, f32[8,64,128]{2,1,0:T(8,128)S(1)}) custom-call(bf16[1024,1024]{1,0:T(8,128)(2,1)} %bitcast.2, s32[3,16]{1,0:T(4,128)} %rp_hbm.1, s32[2,3]{1,0:T(2,128)} %bitcast.3), custom_call_target="tpu_custom_call" | custom-call | tf_op jit(solution)/shard_map/wave_sums/pallas_call | solution.py:172
  2.2 1.5 %collective-permute-start = (f32[8,64,128]{2,1,0:T(8,128)S(1)}, f32[8,64,128]{2,1,0:T(8,128)S(1)}, u32[]{:S(2)}, u32[]{:S(2)}) collective-permute-start(f32[8,64,128]{2,1,0:T(8,128)S(1)} %get-tuple-element.10), channel_id=1, source_target_pairs={{0,1},{1,0},{2,3},{3,2},{4,5},{5,4},{6,7},{7,6},{8,9},{9,8},{10,11... | collective-permute-start | bytes 786440 | tf_op jit(solution)/shard_map/ppermute | solution.py:186
  3.7 0.0 copy-done.1
  3.7 0.0 copy-done
  3.7 1.0 %phases.1.phase_ref = bf16[512,1024]{1,0:T(8,128)(2,1)S(1)} custom-call(s32[3,512]{1,0:T(4,128)S(1)} %copy-done, s32[3,512]{1,0:T(4,128)S(1)} %copy-done.1), custom_call_target="tpu_custom_call" | custom-call | tf_op jit(solution)/shard_map/phases/pallas_call | solution.py:187
  4.7 0.2 collective-permute-done.got_ref
  4.9 14.2 %all_to_all.15.parts_ref = bf16[8,64,128]{2,1,0:T(8,128)(2,1)S(1)} all-to-all(bf16[8,64,128]{2,1,0:T(8,128)(2,1)S(1)} %add_cores.1), channel_id=1, replica_groups={{0,2,4,6,8,10,12,14},{1,3,5,7,9,11,13,15},{16,18,20,22,24,26,28,30},{17..., dimensions={0} | all-to-all | bytes 262144 | tf_op jit(solution)/shard_map/all_to_all | solution.py:202
  19.1 0.1 add_parts.1
  19.1 9.8 %all_to_all.16.mid_ref = s16[8,72,128]{2,1,0:T(8,128)(2,1)S(1)} all-to-all(s16[8,72,128]{2,1,0:T(8,128)(2,1)S(1)} %add_parts.1), channel_id=1, replica_groups=mesh['ka'=8,'rp'=16] {'ka'}, dimensions={0} | all-to-all | bytes 294912 | tf_op jit(solution)/shard_map/all_to_all | solution.py:210
  28.9 0.6 %bloch.1 = s16[16,40,128]{2,1,0:T(8,128)(2,1)S(1)} custom-call(s16[8,72,128]{2,1,0:T(8,128)(2,1)S(1)} %all_to_all.16.mid_ref, bf16[512,1024]{1,0:T(8,128)(2,1)S(1)} %phases.1.phase_ref), custom_call_target="tpu_custom_call" | custom-call | tf_op jit(solution)/shard_map/bloch/pallas_call | solution.py:211
  29.5 14.2 %all_to_all.17.pieces_ref = s16[16,40,128]{2,1,0:T(8,128)(2,1)S(1)} all-to-all(s16[16,40,128]{2,1,0:T(8,128)(2,1)S(1)} %bloch.1), channel_id=1, replica_groups=mesh['ka'=8,'rp'=16] {'rp'}, dimensions={0} | all-to-all | bytes 327680 | tf_op jit(solution)/shard_map/all_to_all | solution.py:218
  43.7 0.8 %place.1 = f32[32,2048]{1,0:T(8,128)} custom-call(s16[16,40,128]{2,1,0:T(8,128)(2,1)S(1)} %all_to_all.17.pieces_ref), custom_call_target="tpu_custom_call" | custom-call | tf_op jit(solution)/shard_map/place/pallas_call | solution.py:219
  (1 shorter events, 0.0 us)
Async XLA Ops:
  0.0 3.7 %copy-start.1 = (s32[3,512]{1,0:T(4,128)S(1)}, s32[3,512]{1,0:T(4,128)}, u32[]{:S(2)}) copy-start(s32[3,512]{1,0:T(4,128)} %re_ref.1) | copy-start | bytes 18436
  0.0 3.7 %copy-start = (s32[3,512]{1,0:T(4,128)S(1)}, s32[3,512]{1,0:T(4,128)}, u32[]{:S(2)}) copy-start(s32[3,512]{1,0:T(4,128)} %k_ref.1) | copy-start | bytes 18436
  2.2 2.7 %collective-permute-start = (f32[8,64,128]{2,1,0:T(8,128)S(1)}, f32[8,64,128]{2,1,0:T(8,128)S(1)}, u32[]{:S(2)}, u32[]{:S(2)}) collective-permute-start(f32[8,64,128]{2,1,0:T(8,128)S(1)} %get-tuple-element.10), channel_id=1, source_target_pairs={{0,1},{1,0},{2,3},{3,2},{4,5},{5,4},{6,7},{7,6},{8,9},{9,8},{10,11... | collective-permute-start | bytes 786440 | tf_op jit(solution)/shard_map/ppermute | solution.py:186

commit v5 on v3

--- a/solution.py
+++ b/solution.py
@@ -10,7 +10,7 @@
 NKG = 16
 LANES = 128
 HALF = 64
-CHUNKS = 4
+CHUNKS = 1
 ROWS = 1024 // CHUNKS
 QUARTER = [math.cos(2.0 * math.pi * n / NKG) for n in range(4)] + [0.0]
 BITS = 14
@@ -98,9 +98,10 @@
     fill_weights(q, rp, weights)
     fill_phases(k, re, phase_ref)
     low = lower_half(16)
-    for g in range(CHUNKS):
-        chunks[g].wait()
-        y = jnp.dot(weights[...], table[ROWS * g : ROWS * (g + 1)], preferred_element_type=jnp.float32)
+    for g in range(4):
+        if (256 * g) % ROWS == 0:
+            chunks[256 * g // ROWS].wait()
+        y = jnp.dot(weights[...], table[256 * g : 256 * (g + 1)], preferred_element_type=jnp.float32)
         y = y[:64] + y[64:]
         by_cos, by_sin = y[:32], y[32:]
         real = by_cos[:, :512] - by_sin[:, 512:]

time: 45.4 us -> 44.6 us (0.982)
  Pallas kernels: 4.63 us -> 3.87 us
    pallas_call x1, Pallas kernels: 3.13 us -> 2.37 us  [per_device(): pl.pallas_call(wave_sums, in_specs=[pl.BlockSpec(memory_space=pl.ANY)] *...]
where the time goes in v5:
time: 44.6 us; the launch traced here: 44.4 us
  blocking collectives  40.5 us (91%)
  Pallas kernels  3.87 us (9%)
    all_to_all x1, blocking collectives, per_device(): parts = lax.all_to_all(parts, 'rp', 0, 0, tiled=True)  17.6 us
    all_to_all x1, blocking collectives, per_device(): pieces = lax.all_to_all(pieces, 'rp', 0, 0, tiled=True)  13.1 us
    all_to_all x1, blocking collectives, per_device(): mid = lax.all_to_all(mid, 'ka', 0, 0, tiled=True)  9.78 us
    pallas_call x1, Pallas kernels, per_device(): pl.pallas_call(wave_sums, in_specs=[pl.BlockSpec(memory_space=pl.ANY)] *...  2.37 us

profile of v5, /device:TPU:1, one launch (start us, length us, event | category | flops | bytes accessed | tf_op | source)
XLA Modules:
  0.0 44.4 jit_solution(7130734188977987846)
XLA Ops:
  0.0 2.4 %wave_sums.1 = (bf16[16,64,128]{2,1,0:T(8,128)(2,1)S(1)}, bf16[512,1024]{1,0:T(8,128)(2,1)S(1)}) custom-call(bf16[1024,1024]{1,0:T(8,128)(2,1)} %bitcast.2, s32[3,512]{1,0:T(4,128)} %k_hbm.1, s32[3,512]{1,0:T(4,128)} %re_hbm.1, s32[3,16]{1,0:T(4,128)} %rp_hbm.1, s32[2,3]{1,0:T(2,128)} %bitcast.3), custom_call_target="tpu_custom_call" | custom-call | tf_op jit(solution)/shard_map/wave_sums/pallas_call | solution.py:167
  2.4 17.6 %all_to_all.15.parts_ref = bf16[16,64,128]{2,1,0:T(8,128)(2,1)S(1)} all-to-all(bf16[16,64,128]{2,1,0:T(8,128)(2,1)S(1)} %get-tuple-element.7), channel_id=1, replica_groups=mesh['ka'=8,'rp'=16] {'rp'}, dimensions={0} | all-to-all | bytes 524288 | tf_op jit(solution)/shard_map/all_to_all | solution.py:183
  20.0 0.1 add_parts.1
  20.1 9.8 %all_to_all.16.mid_ref = s16[8,72,128]{2,1,0:T(8,128)(2,1)S(1)} all-to-all(s16[8,72,128]{2,1,0:T(8,128)(2,1)S(1)} %add_parts.1), channel_id=1, replica_groups=mesh['ka'=8,'rp'=16] {'ka'}, dimensions={0} | all-to-all | bytes 294912 | tf_op jit(solution)/shard_map/all_to_all | solution.py:191
  29.9 0.6 %bloch.1 = s16[16,40,128]{2,1,0:T(8,128)(2,1)S(1)} custom-call(s16[8,72,128]{2,1,0:T(8,128)(2,1)S(1)} %all_to_all.16.mid_ref, bf16[512,1024]{1,0:T(8,128)(2,1)S(1)} %get-tuple-element.8.phase_ref), custom_call_target="tpu_custom_call" | custom-call | tf_op jit(solution)/shard_map/bloch/pallas_call | solution.py:192
  30.4 13.1 %all_to_all.17.pieces_ref = s16[16,40,128]{2,1,0:T(8,128)(2,1)S(1)} all-to-all(s16[16,40,128]{2,1,0:T(8,128)(2,1)S(1)} %bloch.1), channel_id=1, replica_groups=mesh['ka'=8,'rp'=16] {'rp'}, dimensions={0} | all-to-all | bytes 327680 | tf_op jit(solution)/shard_map/all_to_all | solution.py:199
  43.5 0.8 %place.1 = f32[32,2048]{1,0:T(8,128)} custom-call(s16[16,40,128]{2,1,0:T(8,128)(2,1)S(1)} %all_to_all.17.pieces_ref), custom_call_target="tpu_custom_call" | custom-call | tf_op jit(solution)/shard_map/place/pallas_call | solution.py:200

commit v6 on v5

--- a/solution.py
+++ b/solution.py
@@ -11,6 +11,8 @@
 LANES = 128
 HALF = 64
 CHUNKS = 1
+ORDER = [4, 3, 15, 7, 10, 2, 1, 6, 0, 8, 9, 11, 12, 14, 13, 5]
+PLACE = [ORDER.index(r) for r in range(16)]
 ROWS = 1024 // CHUNKS
 QUARTER = [math.cos(2.0 * math.pi * n / NKG) for n in range(4)] + [0.0]
 BITS = 14
@@ -113,8 +115,8 @@
                 im_part = imag[16 * w : 16 * w + 16, LANES * b : LANES * (b + 1)]
                 first = jnp.where(low, re_part, pltpu.roll(im_part, HALF, 1))
                 second = jnp.where(low, pltpu.roll(re_part, HALF, 1), im_part)
-                out_ref[8 * w + 2 * b, rows] = first.astype(out_ref.dtype)
-                out_ref[8 * w + 2 * b + 1, rows] = second.astype(out_ref.dtype)
+                out_ref[PLACE[8 * w + 2 * b], rows] = first.astype(out_ref.dtype)
+                out_ref[PLACE[8 * w + 2 * b + 1], rows] = second.astype(out_ref.dtype)
 
 
 def add_parts(parts_ref, out_ref):
@@ -144,15 +146,15 @@
     out = jnp.dot(phase_ref[...], both, preferred_element_type=jnp.float32)
     packed, header = pack(out[:, :LANES] + out[:, LANES:])
     for r in range(16):
-        out_ref[r, :32] = packed[32 * r : 32 * r + 32]
-        out_ref[r, 32:] = header
+        out_ref[PLACE[r], :32] = packed[32 * r : 32 * r + 32]
+        out_ref[PLACE[r], 32:] = header
 
 
 def place(pieces_ref, out_ref):
     low = lower_half(32)
     for pair in range(8):
-        x0 = unpack(pieces_ref[2 * pair])
-        x1 = unpack(pieces_ref[2 * pair + 1])
+        x0 = unpack(pieces_ref[PLACE[2 * pair]])
+        x1 = unpack(pieces_ref[PLACE[2 * pair + 1]])
         at = LANES * pair
         out_ref[:, at : at + LANES] = jnp.where(low, x0, pltpu.roll(x1, HALF, 1))
         out_ref[:, 1024 + at : 1024 + at + LANES] = jnp.where(low, pltpu.roll(x0, HALF, 1), x1)
@@ -180,7 +182,7 @@
         ],
         name="wave_sums",
     )(coupling_table.reshape(1024, 1024), k_points, re_vectors, rp_vectors, q_points.T)
-    parts = lax.all_to_all(parts, "rp", 0, 0, tiled=True)
+    parts = lax.all_to_all(parts, "rp", 0, 0, axis_index_groups=[ORDER], tiled=True)
     mid = pl.pallas_call(
         add_parts,
         in_specs=[vmem],
@@ -196,7 +198,7 @@
         out_shape=pltpu.VMEM((16, 40, LANES), jnp.int16),
         name="bloch",
     )(in_vmem(mid), in_vmem(phase))
-    pieces = lax.all_to_all(pieces, "rp", 0, 0, tiled=True)
+    pieces = lax.all_to_all(pieces, "rp", 0, 0, axis_index_groups=[ORDER], tiled=True)
     return pl.pallas_call(
         place,
         in_specs=[vmem],

time: 44.6 us -> 42.6 us (0.955)
  blocking collectives: 40.5 us -> 38.4 us
    all_to_all x2, blocking collectives: 30.7 us -> 28.7 us  [the longest x1 16.1 us: per_device(): lax.all_to_all(parts, 'rp', 0, 0, axis_index_groups=[ORDER], tiled=True)]
where the time goes in v6:
time: 42.6 us; the launch traced here: 42.3 us
  blocking collectives  38.4 us (90%)
  Pallas kernels  3.87 us (9%)
    all_to_all x1, blocking collectives, per_device(): lax.all_to_all(parts, 'rp', 0, 0, axis_index_groups=[ORDER], tiled=True)  16.1 us
    all_to_all x1, blocking collectives, per_device(): lax.all_to_all(pieces, 'rp', 0, 0, axis_index_groups=[ORDER], tiled=True)  12.6 us
    all_to_all x1, blocking collectives, per_device(): mid = lax.all_to_all(mid, 'ka', 0, 0, tiled=True)  9.76 us
    pallas_call x1, Pallas kernels, per_device(): pl.pallas_call(wave_sums, in_specs=[pl.BlockSpec(memory_space=pl.ANY)] *...  2.37 us

profile of v6, /device:TPU:1, one launch (start us, length us, event | category | flops | bytes accessed | tf_op | source)
XLA Modules:
  0.0 42.3 jit_solution(2435982103367262462)
XLA Ops:
  0.0 2.4 %wave_sums.1 = (bf16[16,64,128]{2,1,0:T(8,128)(2,1)S(1)}, bf16[512,1024]{1,0:T(8,128)(2,1)S(1)}) custom-call(bf16[1024,1024]{1,0:T(8,128)(2,1)} %bitcast.2, s32[3,512]{1,0:T(4,128)} %k_hbm.1, s32[3,512]{1,0:T(4,128)} %re_hbm.1, s32[3,16]{1,0:T(4,128)} %rp_hbm.1, s32[2,3]{1,0:T(2,128)} %bitcast.3), custom_call_target="tpu_custom_call" | custom-call | tf_op jit(solution)/shard_map/wave_sums/pallas_call | solution.py:169
  2.4 16.1 %all_to_all.15.parts_ref = bf16[16,64,128]{2,1,0:T(8,128)(2,1)S(1)} all-to-all(bf16[16,64,128]{2,1,0:T(8,128)(2,1)S(1)} %get-tuple-element.7), channel_id=1, replica_groups={{4,3,15,7,10,2,1,6,0,8,9,11,12,14,13,5},{20,19,31,23,26,18,17,22,16,24,..., dimensions={0} | all-to-all | bytes 524288 | tf_op jit(solution)/shard_map/all_to_all | solution.py:185
  18.5 0.1 add_parts.1
  18.6 9.8 %all_to_all.16.mid_ref = s16[8,72,128]{2,1,0:T(8,128)(2,1)S(1)} all-to-all(s16[8,72,128]{2,1,0:T(8,128)(2,1)S(1)} %add_parts.1), channel_id=1, replica_groups=mesh['ka'=8,'rp'=16] {'ka'}, dimensions={0} | all-to-all | bytes 294912 | tf_op jit(solution)/shard_map/all_to_all | solution.py:193
  28.3 0.6 %bloch.1 = s16[16,40,128]{2,1,0:T(8,128)(2,1)S(1)} custom-call(s16[8,72,128]{2,1,0:T(8,128)(2,1)S(1)} %all_to_all.16.mid_ref, bf16[512,1024]{1,0:T(8,128)(2,1)S(1)} %get-tuple-element.8.phase_ref), custom_call_target="tpu_custom_call" | custom-call | tf_op jit(solution)/shard_map/bloch/pallas_call | solution.py:194
  28.9 12.6 %all_to_all.17.pieces_ref = s16[16,40,128]{2,1,0:T(8,128)(2,1)S(1)} all-to-all(s16[16,40,128]{2,1,0:T(8,128)(2,1)S(1)} %bloch.1), channel_id=1, replica_groups={{4,3,15,7,10,2,1,6,0,8,9,11,12,14,13,5},{20,19,31,23,26,18,17,22,16,24,..., dimensions={0} | all-to-all | bytes 327680 | tf_op jit(solution)/shard_map/all_to_all | solution.py:201
  41.5 0.8 %place.1 = f32[32,2048]{1,0:T(8,128)} custom-call(s16[16,40,128]{2,1,0:T(8,128)(2,1)S(1)} %all_to_all.17.pieces_ref), custom_call_target="tpu_custom_call" | custom-call | tf_op jit(solution)/shard_map/place/pallas_call | solution.py:202

commit v7 on v5

--- a/solution.py
+++ b/solution.py
@@ -12,6 +12,12 @@
 HALF = 64
 CHUNKS = 1
 ROWS = 1024 // CHUNKS
+ORDER1 = [5, 11, 9, 3, 12, 10, 8, 6, 14, 2, 7, 15, 13, 4, 0, 1]
+ORDER2 = [5, 1, 2, 0, 6, 3, 4, 7]
+ORDER3 = [4, 3, 15, 7, 10, 2, 1, 6, 0, 8, 9, 11, 12, 14, 13, 5]
+PLACE1 = [ORDER1.index(r) for r in range(16)]
+PLACE2 = [ORDER2.index(a) for a in range(8)]
+PLACE3 = [ORDER3.index(r) for r in range(16)]
 QUARTER = [math.cos(2.0 * math.pi * n / NKG) for n in range(4)] + [0.0]
 BITS = 14
 SMALLEST = 2.0**-100
@@ -113,8 +119,8 @@
                 im_part = imag[16 * w : 16 * w + 16, LANES * b : LANES * (b + 1)]
                 first = jnp.where(low, re_part, pltpu.roll(im_part, HALF, 1))
                 second = jnp.where(low, pltpu.roll(re_part, HALF, 1), im_part)
-                out_ref[8 * w + 2 * b, rows] = first.astype(out_ref.dtype)
-                out_ref[8 * w + 2 * b + 1, rows] = second.astype(out_ref.dtype)
+                out_ref[PLACE1[8 * w + 2 * b], rows] = first.astype(out_ref.dtype)
+                out_ref[PLACE1[8 * w + 2 * b + 1], rows] = second.astype(out_ref.dtype)
 
 
 def add_parts(parts_ref, out_ref):
@@ -131,7 +137,7 @@
     straight, turned = [], []
     low = lower_half(64)
     for a in range(8):
-        x = unpack(mid_ref[a])
+        x = unpack(mid_ref[PLACE2[a]])
         high = x.astype(jnp.bfloat16).astype(jnp.float32)
         row, turned_row = [], []
         for piece in (high, x - high):
@@ -144,15 +150,15 @@
     out = jnp.dot(phase_ref[...], both, preferred_element_type=jnp.float32)
     packed, header = pack(out[:, :LANES] + out[:, LANES:])
     for r in range(16):
-        out_ref[r, :32] = packed[32 * r : 32 * r + 32]
-        out_ref[r, 32:] = header
+        out_ref[PLACE3[r], :32] = packed[32 * r : 32 * r + 32]
+        out_ref[PLACE3[r], 32:] = header
 
 
 def place(pieces_ref, out_ref):
     low = lower_half(32)
     for pair in range(8):
-        x0 = unpack(pieces_ref[2 * pair])
-        x1 = unpack(pieces_ref[2 * pair + 1])
+        x0 = unpack(pieces_ref[PLACE3[2 * pair]])
+        x1 = unpack(pieces_ref[PLACE3[2 * pair + 1]])
         at = LANES * pair
         out_ref[:, at : at + LANES] = jnp.where(low, x0, pltpu.roll(x1, HALF, 1))
         out_ref[:, 1024 + at : 1024 + at + LANES] = jnp.where(low, pltpu.roll(x0, HALF, 1), x1)
@@ -180,7 +186,7 @@
         ],
         name="wave_sums",
     )(coupling_table.reshape(1024, 1024), k_points, re_vectors, rp_vectors, q_points.T)
-    parts = lax.all_to_all(parts, "rp", 0, 0, tiled=True)
+    parts = lax.all_to_all(parts, "rp", 0, 0, axis_index_groups=[ORDER1], tiled=True)
     mid = pl.pallas_call(
         add_parts,
         in_specs=[vmem],
@@ -188,7 +194,7 @@
         out_shape=pltpu.VMEM((8, 72, LANES), jnp.int16),
         name="add_parts",
     )(in_vmem(parts))
-    mid = lax.all_to_all(mid, "ka", 0, 0, tiled=True)
+    mid = lax.all_to_all(mid, "ka", 0, 0, axis_index_groups=[ORDER2], tiled=True)
     pieces = pl.pallas_call(
         bloch,
         in_specs=[vmem, vmem],
@@ -196,7 +202,7 @@
         out_shape=pltpu.VMEM((16, 40, LANES), jnp.int16),
         name="bloch",
     )(in_vmem(mid), in_vmem(phase))
-    pieces = lax.all_to_all(pieces, "rp", 0, 0, tiled=True)
+    pieces = lax.all_to_all(pieces, "rp", 0, 0, axis_index_groups=[ORDER3], tiled=True)
     return pl.pallas_call(
         place,
         in_specs=[vmem],

time: 44.6 us -> 40.3 us (0.904)
  blocking collectives: 40.5 us -> 36.1 us
    all_to_all x3, blocking collectives: 40.5 us -> 36.1 us  [the longest x1 16 us: per_device(): lax.all_to_all(parts, 'rp', 0, 0, axis_index_groups=[ORDER1], tiled=True)]
where the time goes in v7:
time: 40.3 us; the launch traced here: 40 us
  blocking collectives  36.1 us (90%)
  Pallas kernels  3.87 us (10%)
    all_to_all x1, blocking collectives, per_device(): lax.all_to_all(parts, 'rp', 0, 0, axis_index_groups=[ORDER1], tiled=True)  16 us
    all_to_all x1, blocking collectives, per_device(): lax.all_to_all(pieces, 'rp', 0, 0, axis_index_groups=[ORDER3], tiled=True)  11.8 us
    all_to_all x1, blocking collectives, per_device(): lax.all_to_all(mid, 'ka', 0, 0, axis_index_groups=[ORDER2], tiled=True)  8.32 us
    pallas_call x1, Pallas kernels, per_device(): pl.pallas_call(wave_sums, in_specs=[pl.BlockSpec(memory_space=pl.ANY)] *...  2.37 us
    pallas_call x1, Pallas kernels, per_device(): pl.pallas_call(place, in_specs=[vmem], out_specs=vmem, out_shape=jax.Shap...  0.85 us

profile of v7, /device:TPU:1, one launch (start us, length us, event | category | flops | bytes accessed | tf_op | source)
XLA Modules:
  0.0 40.0 jit_solution(10859804097100260697)
XLA Ops:
  0.0 2.4 %wave_sums.1 = (bf16[16,64,128]{2,1,0:T(8,128)(2,1)S(1)}, bf16[512,1024]{1,0:T(8,128)(2,1)S(1)}) custom-call(bf16[1024,1024]{1,0:T(8,128)(2,1)} %bitcast.2, s32[3,512]{1,0:T(4,128)} %k_hbm.1, s32[3,512]{1,0:T(4,128)} %re_hbm.1, s32[3,16]{1,0:T(4,128)} %rp_hbm.1, s32[2,3]{1,0:T(2,128)} %bitcast.3), custom_call_target="tpu_custom_call" | custom-call | tf_op jit(solution)/shard_map/wave_sums/pallas_call | solution.py:173
  2.4 16.0 %all_to_all.15.parts_ref = bf16[16,64,128]{2,1,0:T(8,128)(2,1)S(1)} all-to-all(bf16[16,64,128]{2,1,0:T(8,128)(2,1)S(1)} %get-tuple-element.7), channel_id=1, replica_groups={{5,11,9,3,12,10,8,6,14,2,7,15,13,4,0,1},{21,27,25,19,28,26,24,22,30,18,..., dimensions={0} | all-to-all | bytes 524288 | tf_op jit(solution)/shard_map/all_to_all | solution.py:189
  18.3 0.1 add_parts.1
  18.4 8.3 %all_to_all.16.mid_ref = s16[8,72,128]{2,1,0:T(8,128)(2,1)S(1)} all-to-all(s16[8,72,128]{2,1,0:T(8,128)(2,1)S(1)} %add_parts.1), channel_id=1, replica_groups={{80,16,32,0,96,48,64,112},{81,17,33,1,97,49,65,113},{82,18,34,2,98,50,6..., dimensions={0} | all-to-all | bytes 294912 | tf_op jit(solution)/shard_map/all_to_all | solution.py:197
  26.7 0.6 %bloch.1 = s16[16,40,128]{2,1,0:T(8,128)(2,1)S(1)} custom-call(s16[8,72,128]{2,1,0:T(8,128)(2,1)S(1)} %all_to_all.16.mid_ref, bf16[512,1024]{1,0:T(8,128)(2,1)S(1)} %get-tuple-element.8.phase_ref), custom_call_target="tpu_custom_call" | custom-call | tf_op jit(solution)/shard_map/bloch/pallas_call | solution.py:198
  27.3 11.8 %all_to_all.17.pieces_ref = s16[16,40,128]{2,1,0:T(8,128)(2,1)S(1)} all-to-all(s16[16,40,128]{2,1,0:T(8,128)(2,1)S(1)} %bloch.1), channel_id=1, replica_groups={{4,3,15,7,10,2,1,6,0,8,9,11,12,14,13,5},{20,19,31,23,26,18,17,22,16,24,..., dimensions={0} | all-to-all | bytes 327680 | tf_op jit(solution)/shard_map/all_to_all | solution.py:205
  39.2 0.8 %place.1 = f32[32,2048]{1,0:T(8,128)} custom-call(s16[16,40,128]{2,1,0:T(8,128)(2,1)S(1)} %all_to_all.17.pieces_ref), custom_call_target="tpu_custom_call" | custom-call | tf_op jit(solution)/shard_map/place/pallas_call | solution.py:206

commit v8 on v7

--- a/solution.py
+++ b/solution.py
@@ -12,9 +12,9 @@
 HALF = 64
 CHUNKS = 1
 ROWS = 1024 // CHUNKS
-ORDER1 = [5, 11, 9, 3, 12, 10, 8, 6, 14, 2, 7, 15, 13, 4, 0, 1]
-ORDER2 = [5, 1, 2, 0, 6, 3, 4, 7]
-ORDER3 = [4, 3, 15, 7, 10, 2, 1, 6, 0, 8, 9, 11, 12, 14, 13, 5]
+ORDER1 = [13, 12, 15, 14, 11, 10, 9, 8, 5, 4, 7, 6, 3, 2, 1, 0]
+ORDER2 = [5, 4, 3, 2, 7, 6, 1, 0]
+ORDER3 = [13, 5, 12, 4, 15, 7, 14, 6, 11, 3, 10, 2, 9, 1, 8, 0]
 PLACE1 = [ORDER1.index(r) for r in range(16)]
 PLACE2 = [ORDER2.index(a) for a in range(8)]
 PLACE3 = [ORDER3.index(r) for r in range(16)]

time: 40.3 us -> 37.4 us (0.928)
  blocking collectives: 36.1 us -> 33.3 us
    all_to_all x1, blocking collectives: 16 us -> 13.6 us  [per_device(): lax.all_to_all(parts, 'rp', 0, 0, axis_index_groups=[ORDER1], tiled=True)]
where the time goes in v8:
time: 37.4 us; the launch traced here: 37.2 us
  blocking collectives  33.3 us (89%)
  Pallas kernels  3.87 us (10%)
    all_to_all x1, blocking collectives, per_device(): lax.all_to_all(parts, 'rp', 0, 0, axis_index_groups=[ORDER1], tiled=True)  13.6 us
    all_to_all x1, blocking collectives, per_device(): lax.all_to_all(pieces, 'rp', 0, 0, axis_index_groups=[ORDER3], tiled=True)  11.6 us
    all_to_all x1, blocking collectives, per_device(): lax.all_to_all(mid, 'ka', 0, 0, axis_index_groups=[ORDER2], tiled=True)  8.12 us
    pallas_call x1, Pallas kernels, per_device(): pl.pallas_call(wave_sums, in_specs=[pl.BlockSpec(memory_space=pl.ANY)] *...  2.37 us
    pallas_call x1, Pallas kernels, per_device(): pl.pallas_call(place, in_specs=[vmem], out_specs=vmem, out_shape=jax.Shap...  0.85 us

profile of v8, /device:TPU:1, one launch (start us, length us, event | category | flops | bytes accessed | tf_op | source)
XLA Modules:
  0.0 37.2 jit_solution(10818938855208058710)
XLA Ops:
  0.0 2.4 %wave_sums.1 = (bf16[16,64,128]{2,1,0:T(8,128)(2,1)S(1)}, bf16[512,1024]{1,0:T(8,128)(2,1)S(1)}) custom-call(bf16[1024,1024]{1,0:T(8,128)(2,1)} %bitcast.2, s32[3,512]{1,0:T(4,128)} %k_hbm.1, s32[3,512]{1,0:T(4,128)} %re_hbm.1, s32[3,16]{1,0:T(4,128)} %rp_hbm.1, s32[2,3]{1,0:T(2,128)} %bitcast.3), custom_call_target="tpu_custom_call" | custom-call | tf_op jit(solution)/shard_map/wave_sums/pallas_call | solution.py:173
  2.4 13.6 %all_to_all.15.parts_ref = bf16[16,64,128]{2,1,0:T(8,128)(2,1)S(1)} all-to-all(bf16[16,64,128]{2,1,0:T(8,128)(2,1)S(1)} %get-tuple-element.7), channel_id=1, replica_groups={{13,12,15,14,11,10,9,8,5,4,7,6,3,2,1,0},{29,28,31,30,27,26,25,24,21,20,..., dimensions={0} | all-to-all | bytes 524288 | tf_op jit(solution)/shard_map/all_to_all | solution.py:189
  15.9 0.1 add_parts.1
  16.0 8.1 %all_to_all.16.mid_ref = s16[8,72,128]{2,1,0:T(8,128)(2,1)S(1)} all-to-all(s16[8,72,128]{2,1,0:T(8,128)(2,1)S(1)} %add_parts.1), channel_id=1, replica_groups={{80,64,48,32,112,96,16,0},{81,65,49,33,113,97,17,1},{82,66,50,34,114,98..., dimensions={0} | all-to-all | bytes 294912 | tf_op jit(solution)/shard_map/all_to_all | solution.py:197
  24.1 0.6 %bloch.1 = s16[16,40,128]{2,1,0:T(8,128)(2,1)S(1)} custom-call(s16[8,72,128]{2,1,0:T(8,128)(2,1)S(1)} %all_to_all.16.mid_ref, bf16[512,1024]{1,0:T(8,128)(2,1)S(1)} %get-tuple-element.8.phase_ref), custom_call_target="tpu_custom_call" | custom-call | tf_op jit(solution)/shard_map/bloch/pallas_call | solution.py:198
  24.7 11.6 %all_to_all.17.pieces_ref = s16[16,40,128]{2,1,0:T(8,128)(2,1)S(1)} all-to-all(s16[16,40,128]{2,1,0:T(8,128)(2,1)S(1)} %bloch.1), channel_id=1, replica_groups={{13,5,12,4,15,7,14,6,11,3,10,2,9,1,8,0},{29,21,28,20,31,23,30,22,27,19,..., dimensions={0} | all-to-all | bytes 327680 | tf_op jit(solution)/shard_map/all_to_all | solution.py:205
  36.4 0.8 %place.1 = f32[32,2048]{1,0:T(8,128)} custom-call(s16[16,40,128]{2,1,0:T(8,128)(2,1)S(1)} %all_to_all.17.pieces_ref), custom_call_target="tpu_custom_call" | custom-call | tf_op jit(solution)/shard_map/place/pallas_call | solution.py:206

commit v9 on v8

--- a/solution.py
+++ b/solution.py
@@ -12,7 +12,7 @@
 HALF = 64
 CHUNKS = 1
 ROWS = 1024 // CHUNKS
-ORDER1 = [13, 12, 15, 14, 11, 10, 9, 8, 5, 4, 7, 6, 3, 2, 1, 0]
+ORDER1 = [13, 12, 15, 14, 11, 10, 9, 8, 5, 2, 7, 6, 3, 4, 1, 0]
 ORDER2 = [5, 4, 3, 2, 7, 6, 1, 0]
 ORDER3 = [13, 5, 12, 4, 15, 7, 14, 6, 11, 3, 10, 2, 9, 1, 8, 0]
 PLACE1 = [ORDER1.index(r) for r in range(16)]

time: 37.4 us -> 37.4 us (level)
  no operation moved by 1% of the time
where the time goes in v9:
time: 37.4 us; the launch traced here: 37.2 us
  blocking collectives  33.3 us (89%)
  Pallas kernels  3.87 us (10%)
    all_to_all x1, blocking collectives, per_device(): lax.all_to_all(parts, 'rp', 0, 0, axis_index_groups=[ORDER1], tiled=True)  13.6 us
    all_to_all x1, blocking collectives, per_device(): lax.all_to_all(pieces, 'rp', 0, 0, axis_index_groups=[ORDER3], tiled=True)  11.6 us
    all_to_all x1, blocking collectives, per_device(): lax.all_to_all(mid, 'ka', 0, 0, axis_index_groups=[ORDER2], tiled=True)  8.12 us
    pallas_call x1, Pallas kernels, per_device(): pl.pallas_call(wave_sums, in_specs=[pl.BlockSpec(memory_space=pl.ANY)] *...  2.37 us
    pallas_call x1, Pallas kernels, per_device(): pl.pallas_call(place, in_specs=[vmem], out_specs=vmem, out_shape=jax.Shap...  0.85 us

profile of v9, /device:TPU:1, one launch (start us, length us, event | category | flops | bytes accessed | tf_op | source)
XLA Modules:
  0.0 37.2 jit_solution(14568936822695658184)
XLA Ops:
  0.0 2.4 %wave_sums.1 = (bf16[16,64,128]{2,1,0:T(8,128)(2,1)S(1)}, bf16[512,1024]{1,0:T(8,128)(2,1)S(1)}) custom-call(bf16[1024,1024]{1,0:T(8,128)(2,1)} %bitcast.2, s32[3,512]{1,0:T(4,128)} %k_hbm.1, s32[3,512]{1,0:T(4,128)} %re_hbm.1, s32[3,16]{1,0:T(4,128)} %rp_hbm.1, s32[2,3]{1,0:T(2,128)} %bitcast.3), custom_call_target="tpu_custom_call" | custom-call | tf_op jit(solution)/shard_map/wave_sums/pallas_call | solution.py:173
  2.4 13.6 %all_to_all.15.parts_ref = bf16[16,64,128]{2,1,0:T(8,128)(2,1)S(1)} all-to-all(bf16[16,64,128]{2,1,0:T(8,128)(2,1)S(1)} %get-tuple-element.7), channel_id=1, replica_groups={{13,12,15,14,11,10,9,8,5,2,7,6,3,4,1,0},{29,28,31,30,27,26,25,24,21,18,..., dimensions={0} | all-to-all | bytes 524288 | tf_op jit(solution)/shard_map/all_to_all | solution.py:189
  15.9 0.1 add_parts.1
  16.0 8.1 %all_to_all.16.mid_ref = s16[8,72,128]{2,1,0:T(8,128)(2,1)S(1)} all-to-all(s16[8,72,128]{2,1,0:T(8,128)(2,1)S(1)} %add_parts.1), channel_id=1, replica_groups={{80,64,48,32,112,96,16,0},{81,65,49,33,113,97,17,1},{82,66,50,34,114,98..., dimensions={0} | all-to-all | bytes 294912 | tf_op jit(solution)/shard_map/all_to_all | solution.py:197
  24.1 0.6 %bloch.1 = s16[16,40,128]{2,1,0:T(8,128)(2,1)S(1)} custom-call(s16[8,72,128]{2,1,0:T(8,128)(2,1)S(1)} %all_to_all.16.mid_ref, bf16[512,1024]{1,0:T(8,128)(2,1)S(1)} %get-tuple-element.8.phase_ref), custom_call_target="tpu_custom_call" | custom-call | tf_op jit(solution)/shard_map/bloch/pallas_call | solution.py:198
  24.7 11.6 %all_to_all.17.pieces_ref = s16[16,40,128]{2,1,0:T(8,128)(2,1)S(1)} all-to-all(s16[16,40,128]{2,1,0:T(8,128)(2,1)S(1)} %bloch.1), channel_id=1, replica_groups={{13,5,12,4,15,7,14,6,11,3,10,2,9,1,8,0},{29,21,28,20,31,23,30,22,27,19,..., dimensions={0} | all-to-all | bytes 327680 | tf_op jit(solution)/shard_map/all_to_all | solution.py:205
  36.4 0.8 %place.1 = f32[32,2048]{1,0:T(8,128)} custom-call(s16[16,40,128]{2,1,0:T(8,128)(2,1)S(1)} %all_to_all.17.pieces_ref), custom_call_target="tpu_custom_call" | custom-call | tf_op jit(solution)/shard_map/place/pallas_call | solution.py:206

commit v10 on v9

--- a/solution.py
+++ b/solution.py
@@ -14,7 +14,7 @@
 ROWS = 1024 // CHUNKS
 ORDER1 = [13, 12, 15, 14, 11, 10, 9, 8, 5, 2, 7, 6, 3, 4, 1, 0]
 ORDER2 = [5, 4, 3, 2, 7, 6, 1, 0]
-ORDER3 = [13, 5, 12, 4, 15, 7, 14, 6, 11, 3, 10, 2, 9, 1, 8, 0]
+ORDER3 = [13, 2, 7, 0, 3, 5, 9, 4, 8, 11, 12, 1, 14, 15, 10, 6]
 PLACE1 = [ORDER1.index(r) for r in range(16)]
 PLACE2 = [ORDER2.index(a) for a in range(8)]
 PLACE3 = [ORDER3.index(r) for r in range(16)]

time: 37.4 us -> 37.2 us (level)
  no operation moved by 1% of the time
where the time goes in v10:
time: 37.2 us; the launch traced here: 37 us
  blocking collectives  33.1 us (89%)
  Pallas kernels  3.87 us (10%)
    all_to_all x1, blocking collectives, per_device(): lax.all_to_all(parts, 'rp', 0, 0, axis_index_groups=[ORDER1], tiled=True)  13.6 us
    all_to_all x1, blocking collectives, per_device(): lax.all_to_all(pieces, 'rp', 0, 0, axis_index_groups=[ORDER3], tiled=True)  11.4 us
    all_to_all x1, blocking collectives, per_device(): lax.all_to_all(mid, 'ka', 0, 0, axis_index_groups=[ORDER2], tiled=True)  8.12 us
    pallas_call x1, Pallas kernels, per_device(): pl.pallas_call(wave_sums, in_specs=[pl.BlockSpec(memory_space=pl.ANY)] *...  2.37 us
    pallas_call x1, Pallas kernels, per_device(): pl.pallas_call(place, in_specs=[vmem], out_specs=vmem, out_shape=jax.Shap...  0.85 us

profile of v10, /device:TPU:1, one launch (start us, length us, event | category | flops | bytes accessed | tf_op | source)
XLA Modules:
  0.0 37.0 jit_solution(13708910300376014049)
XLA Ops:
  0.0 2.4 %wave_sums.1 = (bf16[16,64,128]{2,1,0:T(8,128)(2,1)S(1)}, bf16[512,1024]{1,0:T(8,128)(2,1)S(1)}) custom-call(bf16[1024,1024]{1,0:T(8,128)(2,1)} %bitcast.2, s32[3,512]{1,0:T(4,128)} %k_hbm.1, s32[3,512]{1,0:T(4,128)} %re_hbm.1, s32[3,16]{1,0:T(4,128)} %rp_hbm.1, s32[2,3]{1,0:T(2,128)} %bitcast.3), custom_call_target="tpu_custom_call" | custom-call | tf_op jit(solution)/shard_map/wave_sums/pallas_call | solution.py:173
  2.4 13.6 %all_to_all.15.parts_ref = bf16[16,64,128]{2,1,0:T(8,128)(2,1)S(1)} all-to-all(bf16[16,64,128]{2,1,0:T(8,128)(2,1)S(1)} %get-tuple-element.7), channel_id=1, replica_groups={{13,12,15,14,11,10,9,8,5,2,7,6,3,4,1,0},{29,28,31,30,27,26,25,24,21,18,..., dimensions={0} | all-to-all | bytes 524288 | tf_op jit(solution)/shard_map/all_to_all | solution.py:189
  15.9 0.1 add_parts.1
  16.0 8.1 %all_to_all.16.mid_ref = s16[8,72,128]{2,1,0:T(8,128)(2,1)S(1)} all-to-all(s16[8,72,128]{2,1,0:T(8,128)(2,1)S(1)} %add_parts.1), channel_id=1, replica_groups={{80,64,48,32,112,96,16,0},{81,65,49,33,113,97,17,1},{82,66,50,34,114,98..., dimensions={0} | all-to-all | bytes 294912 | tf_op jit(solution)/shard_map/all_to_all | solution.py:197
  24.1 0.6 %bloch.1 = s16[16,40,128]{2,1,0:T(8,128)(2,1)S(1)} custom-call(s16[8,72,128]{2,1,0:T(8,128)(2,1)S(1)} %all_to_all.16.mid_ref, bf16[512,1024]{1,0:T(8,128)(2,1)S(1)} %get-tuple-element.8.phase_ref), custom_call_target="tpu_custom_call" | custom-call | tf_op jit(solution)/shard_map/bloch/pallas_call | solution.py:198
  24.7 11.4 %all_to_all.17.pieces_ref = s16[16,40,128]{2,1,0:T(8,128)(2,1)S(1)} all-to-all(s16[16,40,128]{2,1,0:T(8,128)(2,1)S(1)} %bloch.1), channel_id=1, replica_groups={{13,2,7,0,3,5,9,4,8,11,12,1,14,15,10,6},{29,18,23,16,19,21,25,20,24,27,..., dimensions={0} | all-to-all | bytes 327680 | tf_op jit(solution)/shard_map/all_to_all | solution.py:205
  36.2 0.8 %place.1 = f32[32,2048]{1,0:T(8,128)} custom-call(s16[16,40,128]{2,1,0:T(8,128)(2,1)S(1)} %all_to_all.17.pieces_ref), custom_call_target="tpu_custom_call" | custom-call | tf_op jit(solution)/shard_map/place/pallas_call | solution.py:206

commit v11 on v9

--- a/solution.py
+++ b/solution.py
@@ -13,7 +13,7 @@
 CHUNKS = 1
 ROWS = 1024 // CHUNKS
 ORDER1 = [13, 12, 15, 14, 11, 10, 9, 8, 5, 2, 7, 6, 3, 4, 1, 0]
-ORDER2 = [5, 4, 3, 2, 7, 6, 1, 0]
+ORDER2 = [5, 4, 3, 7, 2, 6, 1, 0]
 ORDER3 = [13, 5, 12, 4, 15, 7, 14, 6, 11, 3, 10, 2, 9, 1, 8, 0]
 PLACE1 = [ORDER1.index(r) for r in range(16)]
 PLACE2 = [ORDER2.index(a) for a in range(8)]

time: 37.4 us -> 37.4 us (level)
  no operation moved by 1% of the time
where the time goes in v11:
time: 37.4 us; the launch traced here: 37.2 us
  blocking collectives  33.3 us (89%)
  Pallas kernels  3.87 us (10%)
    all_to_all x1, blocking collectives, per_device(): lax.all_to_all(parts, 'rp', 0, 0, axis_index_groups=[ORDER1], tiled=True)  13.6 us
    all_to_all x1, blocking collectives, per_device(): lax.all_to_all(pieces, 'rp', 0, 0, axis_index_groups=[ORDER3], tiled=True)  11.7 us
    all_to_all x1, blocking collectives, per_device(): lax.all_to_all(mid, 'ka', 0, 0, axis_index_groups=[ORDER2], tiled=True)  8.01 us
    pallas_call x1, Pallas kernels, per_device(): pl.pallas_call(wave_sums, in_specs=[pl.BlockSpec(memory_space=pl.ANY)] *...  2.37 us
    pallas_call x1, Pallas kernels, per_device(): pl.pallas_call(place, in_specs=[vmem], out_specs=vmem, out_shape=jax.Shap...  0.85 us

profile of v11, /device:TPU:1, one launch (start us, length us, event | category | flops | bytes accessed | tf_op | source)
XLA Modules:
  0.0 37.2 jit_solution(14766753717804377880)
XLA Ops:
  0.0 2.4 %wave_sums.1 = (bf16[16,64,128]{2,1,0:T(8,128)(2,1)S(1)}, bf16[512,1024]{1,0:T(8,128)(2,1)S(1)}) custom-call(bf16[1024,1024]{1,0:T(8,128)(2,1)} %bitcast.2, s32[3,512]{1,0:T(4,128)} %k_hbm.1, s32[3,512]{1,0:T(4,128)} %re_hbm.1, s32[3,16]{1,0:T(4,128)} %rp_hbm.1, s32[2,3]{1,0:T(2,128)} %bitcast.3), custom_call_target="tpu_custom_call" | custom-call | tf_op jit(solution)/shard_map/wave_sums/pallas_call | solution.py:173
  2.4 13.6 %all_to_all.15.parts_ref = bf16[16,64,128]{2,1,0:T(8,128)(2,1)S(1)} all-to-all(bf16[16,64,128]{2,1,0:T(8,128)(2,1)S(1)} %get-tuple-element.7), channel_id=1, replica_groups={{13,12,15,14,11,10,9,8,5,2,7,6,3,4,1,0},{29,28,31,30,27,26,25,24,21,18,..., dimensions={0} | all-to-all | bytes 524288 | tf_op jit(solution)/shard_map/all_to_all | solution.py:189
  15.9 0.1 add_parts.1
  16.0 8.0 %all_to_all.16.mid_ref = s16[8,72,128]{2,1,0:T(8,128)(2,1)S(1)} all-to-all(s16[8,72,128]{2,1,0:T(8,128)(2,1)S(1)} %add_parts.1), channel_id=1, replica_groups={{80,64,48,112,32,96,16,0},{81,65,49,113,33,97,17,1},{82,66,50,114,34,98..., dimensions={0} | all-to-all | bytes 294912 | tf_op jit(solution)/shard_map/all_to_all | solution.py:197
  24.0 0.6 %bloch.1 = s16[16,40,128]{2,1,0:T(8,128)(2,1)S(1)} custom-call(s16[8,72,128]{2,1,0:T(8,128)(2,1)S(1)} %all_to_all.16.mid_ref, bf16[512,1024]{1,0:T(8,128)(2,1)S(1)} %get-tuple-element.8.phase_ref), custom_call_target="tpu_custom_call" | custom-call | tf_op jit(solution)/shard_map/bloch/pallas_call | solution.py:198
  24.6 11.7 %all_to_all.17.pieces_ref = s16[16,40,128]{2,1,0:T(8,128)(2,1)S(1)} all-to-all(s16[16,40,128]{2,1,0:T(8,128)(2,1)S(1)} %bloch.1), channel_id=1, replica_groups={{13,5,12,4,15,7,14,6,11,3,10,2,9,1,8,0},{29,21,28,20,31,23,30,22,27,19,..., dimensions={0} | all-to-all | bytes 327680 | tf_op jit(solution)/shard_map/all_to_all | solution.py:205
  36.3 0.8 %place.1 = f32[32,2048]{1,0:T(8,128)} custom-call(s16[16,40,128]{2,1,0:T(8,128)(2,1)S(1)} %all_to_all.17.pieces_ref), custom_call_target="tpu_custom_call" | custom-call | tf_op jit(solution)/shard_map/place/pallas_call | solution.py:206
